TPU v7x, 32 devices: a whole 2x2x4 slice. The times are simulated.
32 devices in a mesh: rep: 8 (over z, core), shard: 4 (over y, x).
Axes of the slice: x: 2, y: 2, z: 4, core: 2. Of those that a mesh axis runs over, the one named last changes fastest.
Arguments:
- tokens: float32 [64, 1024, 768], P(('rep', 'shard')), may hold values from -6 to 6
- segments: int32 [64, 1024], P(('rep', 'shard')), may hold values from 0 to 3, never falling along the last dimension, each value on 1 to 800 neighbouring positions
- time_steps: int32 [64], P(('rep', 'shard')), may hold values from 0 to 1999
- time_table: bfloat16 [2000, 768], P('shard'), may hold values from -4 to 4
- ln1_gain: bfloat16 [768], P('shard'), may hold values from 0.5 to 1.5
- ln1_bias: bfloat16 [768], P('shard'), may hold values from -1 to 1
- q_weight: bfloat16 [768, 768], P('shard'), may hold values from -0.21875 to 0.21875
- q_bias: bfloat16 [768], P('shard'), may hold values from -1 to 1
- k_weight: bfloat16 [768, 768], P('shard'), may hold values from -0.21875 to 0.21875
- v_weight: bfloat16 [768, 768], P('shard'), may hold values from -0.21875 to 0.21875
- v_bias: bfloat16 [768], P('shard'), may hold values from -1 to 1
- o_weight: bfloat16 [768, 768], P('shard'), may hold values from -0.875 to 0.875
- o_bias: bfloat16 [768], P('shard'), may hold values from -1 to 1
- ln2_gain: bfloat16 [768], P('shard'), may hold values from 0.5 to 1.5
- ln2_bias: bfloat16 [768], P('shard'), may hold values from -1 to 1
- up_weight: bfloat16 [768, 3072], P('shard'), may hold values from -0.21875 to 0.21875
- up_bias: bfloat16 [3072], P('shard'), may hold values from -1 to 1
- down_weight: bfloat16 [3072, 768], P('shard'), may hold values from -0.109375 to 0.109375
- down_bias: bfloat16 [768], P('shard'), may hold values from -1 to 1
- cotangent: float32 [64, 1024, 768], P(('rep', 'shard')), may hold values from -6 to 6
Outputs:
- result: float32 [64, 1024, 768], P(('rep', 'shard'))
- grad_tokens: float32 [64, 1024, 768], P(('rep', 'shard'))
- grad_time_table: float32 [2000, 768], P('shard')
- grad_ln1_gain: float32 [768], P('shard')
- grad_ln1_bias: float32 [768], P('shard')
- grad_q_weight: float32 [768, 768], P('shard')
- grad_q_bias: float32 [768], P('shard')
- grad_k_weight: float32 [768, 768], P('shard')
- grad_v_weight: float32 [768, 768], P('shard')
- grad_v_bias: float32 [768], P('shard')
- grad_o_weight: float32 [768, 768], P('shard')
- grad_o_bias: float32 [768], P('shard')
- grad_ln2_gain: float32 [768], P('shard')
- grad_ln2_bias: float32 [768], P('shard')
- grad_up_weight: float32 [768, 3072], P('shard')
- grad_up_bias: float32 [3072], P('shard')
- grad_down_weight: float32 [3072, 768], P('shard')
- grad_down_bias: float32 [768], P('shard')
Inputs may be any that keep to these rules, and one draw needn't show every extreme that they name: `segments`: within a sequence segment numbers never fall; each document holds 1 to 800 tokens and one holds exactly 800.
All inputs are finite; a program needn't handle non-finite values.
Results may differ from a plain program's by a relative error of at most 0.022.
Values may be sent and summed in bfloat16 or wider, within the bound.
No kernel may reach another device: no remote copies, remote signals or barrier semaphores. Data moves between devices by JAX's collectives and lax.ppermute only.
A program may use at most 320 MiB of HBM per device.

v0:
```python
import jax
import jax.numpy as jnp
from jax import lax
from jax.sharding import PartitionSpec as P

HEADS = 12


EPS = 1e-05
NEG = -1e30


def layer_norm(values, gain, shift):
    centre = jnp.mean(values, axis=-1, keepdims=True)
    offsets = values - centre
    spread = jnp.mean(offsets * offsets, axis=-1, keepdims=True)
    return offsets * lax.rsqrt(spread + EPS) * gain + shift


def exact_gelu(values):
    return jax.nn.gelu(values, approximate=False)


def project(left, right):
    return jnp.dot(left, right, preferred_element_type=jnp.float32)


def project_left(left, right):
    return jnp.einsum("ta,tb->ab", left, right, preferred_element_type=jnp.float32)


def project_back(left, right):
    return jnp.einsum("tb,ab->ta", left, right, preferred_element_type=jnp.float32)


def column_sums(values):
    return jnp.sum(values, axis=0, dtype=jnp.float32)


def masked_scores(query_rows, key_heads, seg_rows, segment_ids):
    raw = (
        jnp.einsum("qhd,khd->hqk", query_rows, key_heads, preferred_element_type=jnp.float32)
        * 0.125
    )
    same = seg_rows[:, None] == segment_ids[None, :]
    return jnp.where(same[None], raw, NEG)


def attend_forward(queries, keys, values, segment_ids, head_count):
    length, width = queries.shape
    size = width // head_count
    q_heads = queries.reshape(length, head_count, size)
    k_heads = keys.reshape(length, head_count, size)
    v_heads = values.reshape(length, head_count, size)
    span = min(512, length)
    outputs = []
    logsums = []
    for offset in range(0, length, span):
        scores = masked_scores(
            q_heads[offset : offset + span],
            k_heads,
            segment_ids[offset : offset + span],
            segment_ids,
        )
        highest = jnp.max(scores, axis=-1, keepdims=True)
        exponent = jnp.exp(scores - highest)
        totals = jnp.sum(exponent, axis=-1, keepdims=True)
        chance = (exponent / totals).astype(jnp.bfloat16)
        logsums.append(highest + jnp.log(totals))
        mixed = jnp.einsum("hqk,khd->qhd", chance, v_heads, preferred_element_type=jnp.float32)
        outputs.append(mixed.reshape(span, width))
    return (jnp.concatenate(outputs, 0).astype(jnp.bfloat16), jnp.concatenate(logsums, 1))


def attend_backward(queries, keys, values, segment_ids, logsums, grad_attended, head_count):
    length, width = queries.shape
    size = width // head_count
    q_heads = queries.reshape(length, head_count, size)
    k_heads = keys.reshape(length, head_count, size)
    v_heads = values.reshape(length, head_count, size)
    grad_heads = grad_attended.reshape(length, head_count, size)
    span = min(512, length)
    grad_keys = jnp.zeros((length, head_count, size), jnp.float32)
    grad_values = jnp.zeros((length, head_count, size), jnp.float32)
    query_parts = []
    for offset in range(0, length, span):
        query_rows = q_heads[offset : offset + span]
        scores = masked_scores(
            query_rows, k_heads, segment_ids[offset : offset + span], segment_ids
        )
        chance = jnp.exp(scores - logsums[:, offset : offset + span])
        grad_rows = grad_heads[offset : offset + span]
        grad_chance = jnp.einsum(
            "qhd,khd->hqk", grad_rows, v_heads, preferred_element_type=jnp.float32
        )
        grad_values = grad_values + jnp.einsum(
            "hqk,qhd->khd",
            chance.astype(jnp.bfloat16),
            grad_rows,
            preferred_element_type=jnp.float32,
        )
        grad_scores = (
            chance * (grad_chance - jnp.sum(chance * grad_chance, axis=-1, keepdims=True))
        ).astype(jnp.bfloat16)
        part = (
            jnp.einsum("hqk,khd->qhd", grad_scores, k_heads, preferred_element_type=jnp.float32)
            * 0.125
        )
        query_parts.append(part.reshape(span, width))
        grad_keys = (
            grad_keys
            + jnp.einsum(
                "hqk,qhd->khd", grad_scores, query_rows, preferred_element_type=jnp.float32
            )
            * 0.125
        )
    grad_queries = jnp.concatenate(query_parts, 0).astype(jnp.bfloat16)
    return (
        grad_queries,
        grad_keys.reshape(length, width).astype(jnp.bfloat16),
        grad_values.reshape(length, width).astype(jnp.bfloat16),
    )


def local(
    tokens,
    segments,
    time_steps,
    time_table,
    ln1_gain,
    ln1_bias,
    q_weight,
    q_bias,
    k_weight,
    v_weight,
    v_bias,
    o_weight,
    o_bias,
    ln2_gain,
    ln2_bias,
    up_weight,
    up_bias,
    down_weight,
    down_bias,
    cotangent,
):
    owned = (
        time_table,
        ln1_gain,
        ln1_bias,
        q_weight,
        q_bias,
        k_weight,
        v_weight,
        v_bias,
        o_weight,
        o_bias,
        ln2_gain,
        ln2_bias,
        up_weight,
        up_bias,
        down_weight,
        down_bias,
    )
    start_totals = tuple((jnp.zeros(item.shape, jnp.float32) for item in owned))

    def one_batch(totals, batch):
        rows, segment_ids, step_index, grad_out = batch
        (
            table_full,
            gain_one,
            shift_one,
            w_query,
            b_query,
            w_key,
            w_value,
            b_value,
            w_out,
            b_out,
            gain_two,
            shift_two,
            w_up,
            b_up,
            w_down,
            b_down,
        ) = (
            lax.all_gather(time_table, "shard", axis=0, tiled=True),
            lax.all_gather(ln1_gain, "shard", axis=0, tiled=True),
            lax.all_gather(ln1_bias, "shard", axis=0, tiled=True),
            lax.all_gather(q_weight, "shard", axis=0, tiled=True),
            lax.all_gather(q_bias, "shard", axis=0, tiled=True),
            lax.all_gather(k_weight, "shard", axis=0, tiled=True),
            lax.all_gather(v_weight, "shard", axis=0, tiled=True),
            lax.all_gather(v_bias, "shard", axis=0, tiled=True),
            lax.all_gather(o_weight, "shard", axis=0, tiled=True),
            lax.all_gather(o_bias, "shard", axis=0, tiled=True),
            lax.all_gather(ln2_gain, "shard", axis=0, tiled=True),
            lax.all_gather(ln2_bias, "shard", axis=0, tiled=True),
            lax.all_gather(up_weight, "shard", axis=0, tiled=True),
            lax.all_gather(up_bias, "shard", axis=0, tiled=True),
            lax.all_gather(down_weight, "shard", axis=0, tiled=True),
            lax.all_gather(down_bias, "shard", axis=0, tiled=True),
        )
        step_row = lax.dynamic_slice_in_dim(table_full, step_index, 1, 0).astype(jnp.float32)
        gain_one_f = gain_one.astype(jnp.float32)
        gain_two_f = gain_two.astype(jnp.float32)
        embedded = rows + step_row
        normed1 = layer_norm(embedded, gain_one_f, shift_one.astype(jnp.float32)).astype(
            jnp.bfloat16
        )
        queries = (project(normed1, w_query) + b_query.astype(jnp.float32)).astype(jnp.bfloat16)
        keys = project(normed1, w_key).astype(jnp.bfloat16)
        values = (project(normed1, w_value) + b_value.astype(jnp.float32)).astype(jnp.bfloat16)
        attended, logsums = attend_forward(queries, keys, values, segment_ids, HEADS)
        mixed1 = embedded + project(attended, w_out) + b_out.astype(jnp.float32)
        normed2 = layer_norm(mixed1, gain_two_f, shift_two.astype(jnp.float32)).astype(jnp.bfloat16)
        pre_act = project(normed2, w_up) + b_up.astype(jnp.float32)
        activated = exact_gelu(pre_act).astype(jnp.bfloat16)
        result = mixed1 + project(activated, w_down) + b_down.astype(jnp.float32)
        (
            back_gain_one,
            back_query,
            back_key,
            back_value,
            back_out,
            back_gain_two,
            back_up,
            back_down,
        ) = (
            lax.all_gather(ln1_gain, "shard", axis=0, tiled=True),
            lax.all_gather(q_weight, "shard", axis=0, tiled=True),
            lax.all_gather(k_weight, "shard", axis=0, tiled=True),
            lax.all_gather(v_weight, "shard", axis=0, tiled=True),
            lax.all_gather(o_weight, "shard", axis=0, tiled=True),
            lax.all_gather(ln2_gain, "shard", axis=0, tiled=True),
            lax.all_gather(up_weight, "shard", axis=0, tiled=True),
            lax.all_gather(down_weight, "shard", axis=0, tiled=True),
        )
        back_gain_one = back_gain_one.astype(jnp.float32)
        back_gain_two = back_gain_two.astype(jnp.float32)
        grad_out_low = grad_out.astype(jnp.bfloat16)
        grad_down_bias = column_sums(grad_out_low)
        grad_down_weight = project_left(activated, grad_out_low)
        grad_act = project_back(grad_out_low, back_down)
        _, gelu_pullback = jax.vjp(exact_gelu, pre_act)
        grad_pre = gelu_pullback(grad_act)[0].astype(jnp.bfloat16)
        grad_up_bias = column_sums(grad_pre)
        grad_up_weight = project_left(normed2, grad_pre)
        grad_normed2 = project_back(grad_pre, back_up)
        _, norm_pullback_two = jax.vjp(
            layer_norm, mixed1, back_gain_two, shift_two.astype(jnp.float32)
        )
        grad_mixed_norm, grad_gain_two, grad_shift_two = norm_pullback_two(grad_normed2)
        grad_mixed1 = grad_out + grad_mixed_norm
        grad_mix_low = grad_mixed1.astype(jnp.bfloat16)
        grad_out_bias = column_sums(grad_mix_low)
        grad_out_weight = project_left(attended, grad_mix_low)
        grad_attended = project_back(grad_mix_low, back_out).astype(jnp.bfloat16)
        grad_queries, grad_keys, grad_values = attend_backward(
            queries, keys, values, segment_ids, logsums, grad_attended, HEADS
        )
        grad_query_bias = column_sums(grad_queries)
        grad_value_bias = column_sums(grad_values)
        grad_query_weight = project_left(normed1, grad_queries)
        grad_key_weight = project_left(normed1, grad_keys)
        grad_value_weight = project_left(normed1, grad_values)
        grad_normed1 = (
            project_back(grad_queries, back_query)
            + project_back(grad_keys, back_key)
            + project_back(grad_values, back_value)
        )
        _, norm_pullback_one = jax.vjp(
            layer_norm, embedded, back_gain_one, shift_one.astype(jnp.float32)
        )
        grad_embed_norm, grad_gain_one, grad_shift_one = norm_pullback_one(grad_normed1)
        grad_tokens = grad_mixed1 + grad_embed_norm
        token_total = jnp.sum(grad_tokens, axis=0)
        picked = (lax.iota(jnp.int32, table_full.shape[0]) == step_index).astype(jnp.float32)
        grad_table = picked[:, None] * token_total[None, :]
        owner_terms = (
            lax.psum_scatter(
                grad_table.astype(jnp.bfloat16), "shard", scatter_dimension=0, tiled=True
            ).astype(jnp.float32),
            lax.psum_scatter(
                grad_gain_one.astype(jnp.bfloat16), "shard", scatter_dimension=0, tiled=True
            ).astype(jnp.float32),
            lax.psum_scatter(
                grad_shift_one.astype(jnp.bfloat16), "shard", scatter_dimension=0, tiled=True
            ).astype(jnp.float32),
            lax.psum_scatter(
                grad_query_weight.astype(jnp.bfloat16), "shard", scatter_dimension=0, tiled=True
            ).astype(jnp.float32),
            lax.psum_scatter(
                grad_query_bias.astype(jnp.bfloat16), "shard", scatter_dimension=0, tiled=True
            ).astype(jnp.float32),
            lax.psum_scatter(
                grad_key_weight.astype(jnp.bfloat16), "shard", scatter_dimension=0, tiled=True
            ).astype(jnp.float32),
            lax.psum_scatter(
                grad_value_weight.astype(jnp.bfloat16), "shard", scatter_dimension=0, tiled=True
            ).astype(jnp.float32),
            lax.psum_scatter(
                grad_value_bias.astype(jnp.bfloat16), "shard", scatter_dimension=0, tiled=True
            ).astype(jnp.float32),
            lax.psum_scatter(
                grad_out_weight.astype(jnp.bfloat16), "shard", scatter_dimension=0, tiled=True
            ).astype(jnp.float32),
            lax.psum_scatter(
                grad_out_bias.astype(jnp.bfloat16), "shard", scatter_dimension=0, tiled=True
            ).astype(jnp.float32),
            lax.psum_scatter(
                grad_gain_two.astype(jnp.bfloat16), "shard", scatter_dimension=0, tiled=True
            ).astype(jnp.float32),
            lax.psum_scatter(
                grad_shift_two.astype(jnp.bfloat16), "shard", scatter_dimension=0, tiled=True
            ).astype(jnp.float32),
            lax.psum_scatter(
                grad_up_weight.astype(jnp.bfloat16), "shard", scatter_dimension=0, tiled=True
            ).astype(jnp.float32),
            lax.psum_scatter(
                grad_up_bias.astype(jnp.bfloat16), "shard", scatter_dimension=0, tiled=True
            ).astype(jnp.float32),
            lax.psum_scatter(
                grad_down_weight.astype(jnp.bfloat16), "shard", scatter_dimension=0, tiled=True
            ).astype(jnp.float32),
            lax.psum_scatter(
                grad_down_bias.astype(jnp.bfloat16), "shard", scatter_dimension=0, tiled=True
            ).astype(jnp.float32),
        )
        new_totals = tuple((total + term for total, term in zip(totals, owner_terms)))
        return (new_totals, (result, grad_tokens))

    totals, (results, grads_in) = lax.scan(
        one_batch, start_totals, (tokens, segments, time_steps, cotangent)
    )
    totals = (
        lax.psum(totals[0].astype(jnp.bfloat16), "rep").astype(jnp.float32),
        lax.psum(totals[1].astype(jnp.bfloat16), "rep").astype(jnp.float32),
        lax.psum(totals[2].astype(jnp.bfloat16), "rep").astype(jnp.float32),
        lax.psum(totals[3].astype(jnp.bfloat16), "rep").astype(jnp.float32),
        lax.psum(totals[4].astype(jnp.bfloat16), "rep").astype(jnp.float32),
        lax.psum(totals[5].astype(jnp.bfloat16), "rep").astype(jnp.float32),
        lax.psum(totals[6].astype(jnp.bfloat16), "rep").astype(jnp.float32),
        lax.psum(totals[7].astype(jnp.bfloat16), "rep").astype(jnp.float32),
        lax.psum(totals[8].astype(jnp.bfloat16), "rep").astype(jnp.float32),
        lax.psum(totals[9].astype(jnp.bfloat16), "rep").astype(jnp.float32),
        lax.psum(totals[10].astype(jnp.bfloat16), "rep").astype(jnp.float32),
        lax.psum(totals[11].astype(jnp.bfloat16), "rep").astype(jnp.float32),
        lax.psum(totals[12].astype(jnp.bfloat16), "rep").astype(jnp.float32),
        lax.psum(totals[13].astype(jnp.bfloat16), "rep").astype(jnp.float32),
        lax.psum(totals[14].astype(jnp.bfloat16), "rep").astype(jnp.float32),
        lax.psum(totals[15].astype(jnp.bfloat16), "rep").astype(jnp.float32),
    )
    return (
        results,
        grads_in,
        totals[0],
        totals[1],
        totals[2],
        totals[3],
        totals[4],
        totals[5],
        totals[6],
        totals[7],
        totals[8],
        totals[9],
        totals[10],
        totals[11],
        totals[12],
        totals[13],
        totals[14],
        totals[15],
    )


def solution(mesh):
    return jax.shard_map(
        local,
        mesh=mesh,
        in_specs=(
            P(("rep", "shard"), None, None),
            P(("rep", "shard"), None),
            P(("rep", "shard")),
            P("shard", None),
            P("shard"),
            P("shard"),
            P("shard", None),
            P("shard"),
            P("shard", None),
            P("shard", None),
            P("shard"),
            P("shard", None),
            P("shard"),
            P("shard"),
            P("shard"),
            P("shard", None),
            P("shard"),
            P("shard", None),
            P("shard"),
            P(("rep", "shard"), None, None),
        ),
        out_specs=(
            P(("rep", "shard"), None, None),
            P(("rep", "shard"), None, None),
            P("shard", None),
            P("shard"),
            P("shard"),
            P("shard", None),
            P("shard"),
            P("shard", None),
            P("shard", None),
            P("shard"),
            P("shard", None),
            P("shard"),
            P("shard"),
            P("shard"),
            P("shard", None),
            P("shard"),
            P("shard", None),
            P("shard"),
        ),
        check_vma=False,
    )
```

profile of v0, /device:TPU:0, one launch (start us, length us, event | category | flops | bytes accessed | tf_op | source)
XLA Modules:
  0.0 1461.8 jit_solution(12689732626441924734)
XLA Ops:
  8.2 1320.5 %while.48 = (s32[]{:T(128)}, f32[500,768]{1,0:T(8,128)}, f32[192]{0:T(256)}, f32[192]{0:T(256)}, f32[192,768]{1,0:T(8,128)}, /*index=5*/f32[192]{0:T(256)}, f32[...) while((s32[]{:T(128)}, f32[500,768]{1,0:T(8,128)}, ...), condition=%wide.region_42.43_spmd.clone, body=%wide.region_0.42_spmd.clone.sunk | while | flops 53859160064 | bytes 1549399936 | solution.py:333
  18.5 17.8 %all-reduce.35 = (bf16[768]{0:T(1024)(128)(2,1)S(1)}, bf16[768]{0:T(1024)(128)(2,1)S(1)}, bf16[768]{0:T(1024)(128)(2,1)S(1)}, bf16[768]{0:T(1024)(128)(2,1)S(1)}...) all-reduce(bf16[768]{0:T(1024)(128)(2,1)S(1)} %dynamic-update-slice, ...), channel_id=1, replica_groups=mesh['rep'=8,'shard'=4] {'shard'}, use_global_device_ids=true, to_apply=%add.4 | all-reduce | flops 5376 | bytes 21504 | tf_op jit(solution)/shard_map/while
  38.2 7.3 all-gather.6
  70.0 18.0 %all-gather.24.cloned.1.call-done = bf16[768,768]{1,0:T(8,128)(2,1)} async-done(((bf16[192,768]{1,0:T(8,128)(2,1)}), bf16[768,768]{1,0:T(8,128)(2,1)}) %all-gather.24.cloned.1.call-update) | async-done | bytes 1179664 | tf_op jit(solution)/shard_map/while/body/eval_jaxpr/all_gather | solution.py:190
  92.5 25.3 %all-gather.26.cloned.1.call-done = bf16[768,768]{1,0:T(8,128)(2,1)} async-done(((bf16[192,768]{1,0:T(8,128)(2,1)}), bf16[768,768]{1,0:T(8,128)(2,1)}) %all-gather.26.cloned.1.call-update) | async-done | bytes 1179664 | tf_op jit(solution)/shard_map/while/body/eval_jaxpr/all_gather | solution.py:192
  121.0 11.0 fusion.252
  132.0 11.8 fusion.253
  150.6 13.7 fusion.254
  164.3 10.7 fusion.249
  175.0 12.6 fusion.250
  191.6 9.6 fusion.251
  206.8 29.1 %all-gather.16.cloned.1.call-done = bf16[768,3072]{1,0:T(8,128)(2,1)} async-done(((bf16[192,3072]{1,0:T(8,128)(2,1)}), bf16[768,3072]{1,0:T(8,128)(2,1)}) %all-gather.16.cloned.1.call-update) | async-done | bytes 4718608 | tf_op jit(solution)/shard_map/while/body/eval_jaxpr/all_gather | solution.py:199
  235.8 38.4 %multiply_convert_fusion.12 = (bf16[1024,3072]{1,0:T(8,128)(2,1)}, f32[1024,3072]{1,0:T(8,128)}, f32[1024,3072]{1,0:T(8,128)}) fusion(f32[3072]{0:T(1024)S(1)} %bitcast.326, bf16[768,3072]{1,0:T(8,128)(2,1)} %all-gather.16.cloned.1.call-done, f32[1024,768]{0,1:T(8,128)} %copy-done.4, f32[768]{0:T(1024)S(1)} %copy-done.71, f32[768]{0:T(1024)S(1)} %copy-done.58, ...), kind=kOutput, calls=%fused_computation.20.clone.1 | convolution fusion | flops 5043388416 | bytes 39348224 | tf_op jit(solution)/shard_map/while/body/eval_jaxpr/dot_general | solution.py:25
  274.3 20.7 %all-gather.28.cloned.1.call-done = bf16[3072,768]{1,0:T(8,128)(2,1)} async-done(((bf16[768,768]{1,0:T(8,128)(2,1)}), bf16[3072,768]{1,0:T(8,128)(2,1)}) %all-gather.28.cloned.1.call-update) | async-done | bytes 4718608 | tf_op jit(solution)/shard_map/while/body/eval_jaxpr/all_gather | solution.py:237
  294.9 17.7 %fusion.257 = (bf16[3072]{0:T(1024)(128)(2,1)}, bf16[1024,3072]{1,0:T(8,128)(2,1)}) fusion(f32[1024,3072]{1,0:T(8,128)} %get-tuple-element.1386, bf16[3072,768]{1,0:T(8,128)(2,1)} %all-gather.28.cloned.1.call-done, f32[1024,3072]{1,0:T(8,128)} %get-tuple-element.1387, f32[3072]{0:T(1024)S(1)} %bitcast.327, f32[1,1024,768]{1,2,0:T(8,128)S(1)} %copy-done.16), kind=kOutput, calls=%fused_computation.150.clone.1 | convolution fusion | flops 4882166784 | bytes 39340032 | tf_op jit(solution)/shard_map/while/body/eval_jaxpr/tb,ab->ta/dot_general | solution.py:33
  312.6 10.4 fusion.258
  341.8 13.8 fusion.260
  355.5 18.5 %multiply_reduce_fusion.20 = (f32[12,512]{1,0:T(8,128)S(1)}, f32[12,512,1024]{2,1,0:T(8,128)}) fusion(f32[12,512]{1,0:T(8,128)S(1)} %copy-done.48, f32[12,512,1024]{2,1,0:T(8,128)} %get-tuple-element.1381, pred[512,1024]{1,0:T(8,128)(4,1)} %get-tuple-element.1378, bf16[512,12,64]{0,2,1:T(8,128)(2,1)} %bitcast.316, bf16[1024,12,64]{0,2,1:T(8,128)(2,1)} %bitcast.310), kind=kOutput, calls=%fused_computation.4.clone.1 | convolution fusion | flops 836757504 | bytes 53264384 | tf_op jit(solution)/shard_map/while/body/eval_jaxpr/qhd,khd->hqk/dot_general | solution.py:93
  374.0 13.2 bitcast_reduce_fusion.6
  390.8 18.6 %multiply_reduce_fusion.19 = (f32[12,512]{1,0:T(8,128)S(1)}, f32[12,512,1024]{2,1,0:T(8,128)}) fusion(f32[12,512]{1,0:T(8,128)S(1)} %copy-done.49, f32[12,512,1024]{2,1,0:T(8,128)} %get-tuple-element.1377, pred[512,1024]{1,0:T(8,128)(4,1)} %get-tuple-element.1373, bf16[512,12,64]{0,2,1:T(8,128)(2,1)} %bitcast.315, bf16[1024,12,64]{0,2,1:T(8,128)(2,1)} %bitcast.311), kind=kOutput, calls=%fused_computation.1.clone.1 | convolution fusion | flops 836757504 | bytes 53264384 | tf_op jit(solution)/shard_map/while/body/eval_jaxpr/qhd,khd->hqk/dot_general | solution.py:93
  409.6 23.9 %multiply_convert_fusion.14 = bf16[12,512,1024]{2,1,0:T(8,128)(2,1)} fusion(f32[12,512,1024]{2,1,0:T(8,128)} %get-tuple-element.1399, f32[12,512]{1,0:T(8,128)S(1)} %get-tuple-element.1400, f32[12,512]{1,0:T(8,128)S(1)} %copy-done.48, f32[12,512,1024]{2,1,0:T(8,128)} %get-tuple-element.1381, pred[512,1024]{1,0:T(8,128)(4,1)} %get-tuple-element.1378), kind=kLoop, calls=%fused_computation.3.clone.1 | loop fusion | flops 37748736 | bytes 63488000 | tf_op jit(solution)/shard_map/while/body/eval_jaxpr/convert_element_type | solution.py:104
  437.9 15.9 %multiply_convert_fusion.13 = bf16[12,512,1024]{2,1,0:T(8,128)(2,1)} fusion(f32[12,512,1024]{2,1,0:T(8,128)} %get-tuple-element.1396, f32[12,512]{1,0:T(8,128)S(1)} %get-tuple-element.1397, f32[12,512]{1,0:T(8,128)S(1)} %copy-done.49, f32[12,512,1024]{2,1,0:T(8,128)S(1)} %bitcast.299, pred[512,1024]{1,0:T(8,128)(4,1)} %get-tuple-element.1373), kind=kLoop, calls=%fused_computation.clone.1 | loop fusion | flops 37748736 | bytes 63488000 | tf_op jit(solution)/shard_map/while/body/eval_jaxpr/convert_element_type | solution.py:104
  453.8 7.3 fusion.262
  468.5 9.2 bitcast_reduce_fusion.8
  477.7 9.2 bitcast_reduce_fusion.7
  490.3 9.8 convolution_convert_fusion.21
  512.0 15.7 %all-reduce.36 = (bf16[768]{0:T(1024)(128)(2,1)S(1)}, bf16[768]{0:T(1024)(128)(2,1)S(1)}, bf16[768]{0:T(1024)(128)(2,1)S(1)}, bf16[768]{0:T(1024)(128)(2,1)S(1)}...) all-reduce(bf16[768]{0:T(1024)(128)(2,1)S(1)} %get-tuple-element.14, ...), channel_id=3, replica_groups=mesh['rep'=8,'shard'=4] {'shard'}, use_global_device_ids=true, to_apply=%region_18.18.clone | all-reduce | flops 9984 | bytes 39936 | tf_op jit(solution)/shard_map/while
  527.6 9.7 fusion.269
  537.3 11.1 add_bitcast_fusion.2
  557.5 63.0 %fusion.267 = bf16[512,768]{1,0:T(8,128)(2,1)} fusion(bf16[2000,768]{1,0:T(8,128)(2,1)S(1)} %multiply_convert_fusion.16), kind=kCustom, calls=%all-reduce-scatter.clone.1 | all-reduce-scatter fusion | flops 1572865 | bytes 3858944 | tf_op jit(solution)/shard_map/while
  646.9 18.8 %reduce-scatter.19.cloned.1.call-done = bf16[768,768]{1,0:T(8,128)(2,1)} async-done(((bf16[3072,768]{1,0:T(8,128)(2,1)}), bf16[768,768]{1,0:T(8,128)(2,1)}) %reduce-scatter.19.cloned.1.call-update) | async-done | bytes 1179664 | tf_op jit(solution)/shard_map/while/body/eval_jaxpr/reduce_scatter | solution.py:323
  678.8 15.4 %all-reduce.35 = (bf16[768]{0:T(1024)(128)(2,1)S(1)}, bf16[768]{0:T(1024)(128)(2,1)S(1)}, bf16[768]{0:T(1024)(128)(2,1)S(1)}, bf16[768]{0:T(1024)(128)(2,1)S(1)}...) all-reduce(bf16[768]{0:T(1024)(128)(2,1)S(1)} %dynamic-update-slice, ...), channel_id=1, replica_groups=mesh['rep'=8,'shard'=4] {'shard'}, use_global_device_ids=true, to_apply=%add.4 | all-reduce | flops 5376 | bytes 21504 | tf_op jit(solution)/shard_map/while
  696.1 8.1 all-gather.6
  704.8 5.8 constant_dynamic-slice_fusion.7
  728.7 16.9 %all-gather.24.cloned.1.call-done = bf16[768,768]{1,0:T(8,128)(2,1)} async-done(((bf16[192,768]{1,0:T(8,128)(2,1)}), bf16[768,768]{1,0:T(8,128)(2,1)}) %all-gather.24.cloned.1.call-update) | async-done | bytes 1179664 | tf_op jit(solution)/shard_map/while/body/eval_jaxpr/all_gather | solution.py:190
  750.0 25.1 %all-gather.26.cloned.1.call-done = bf16[768,768]{1,0:T(8,128)(2,1)} async-done(((bf16[192,768]{1,0:T(8,128)(2,1)}), bf16[768,768]{1,0:T(8,128)(2,1)}) %all-gather.26.cloned.1.call-update) | async-done | bytes 1179664 | tf_op jit(solution)/shard_map/while/body/eval_jaxpr/all_gather | solution.py:192
  778.5 11.0 fusion.252
  789.4 11.8 fusion.253
  808.0 13.7 fusion.254
  821.7 10.7 fusion.249
  832.4 12.5 fusion.250
  849.0 9.6 fusion.251
  864.2 29.2 %all-gather.16.cloned.1.call-done = bf16[768,3072]{1,0:T(8,128)(2,1)} async-done(((bf16[192,3072]{1,0:T(8,128)(2,1)}), bf16[768,3072]{1,0:T(8,128)(2,1)}) %all-gather.16.cloned.1.call-update) | async-done | bytes 4718608 | tf_op jit(solution)/shard_map/while/body/eval_jaxpr/all_gather | solution.py:199
  893.4 38.4 %multiply_convert_fusion.12 = (bf16[1024,3072]{1,0:T(8,128)(2,1)}, f32[1024,3072]{1,0:T(8,128)}, f32[1024,3072]{1,0:T(8,128)}) fusion(f32[3072]{0:T(1024)S(1)} %bitcast.326, bf16[768,3072]{1,0:T(8,128)(2,1)} %all-gather.16.cloned.1.call-done, f32[1024,768]{0,1:T(8,128)} %copy-done.4, f32[768]{0:T(1024)S(1)} %copy-done.71, f32[768]{0:T(1024)S(1)} %copy-done.58, ...), kind=kOutput, calls=%fused_computation.20.clone.1 | convolution fusion | flops 5043388416 | bytes 39348224 | tf_op jit(solution)/shard_map/while/body/eval_jaxpr/dot_general | solution.py:25
  931.9 20.5 %all-gather.28.cloned.1.call-done = bf16[3072,768]{1,0:T(8,128)(2,1)} async-done(((bf16[768,768]{1,0:T(8,128)(2,1)}), bf16[3072,768]{1,0:T(8,128)(2,1)}) %all-gather.28.cloned.1.call-update) | async-done | bytes 4718608 | tf_op jit(solution)/shard_map/while/body/eval_jaxpr/all_gather | solution.py:237
  952.4 17.7 %fusion.257 = (bf16[3072]{0:T(1024)(128)(2,1)}, bf16[1024,3072]{1,0:T(8,128)(2,1)}) fusion(f32[1024,3072]{1,0:T(8,128)} %get-tuple-element.1386, bf16[3072,768]{1,0:T(8,128)(2,1)} %all-gather.28.cloned.1.call-done, f32[1024,3072]{1,0:T(8,128)} %get-tuple-element.1387, f32[3072]{0:T(1024)S(1)} %bitcast.327, f32[1,1024,768]{1,2,0:T(8,128)S(1)} %copy-done.16), kind=kOutput, calls=%fused_computation.150.clone.1 | convolution fusion | flops 4882166784 | bytes 39340032 | tf_op jit(solution)/shard_map/while/body/eval_jaxpr/tb,ab->ta/dot_general | solution.py:33
  970.0 10.4 fusion.258
  999.2 13.8 fusion.260
  1013.0 18.5 %multiply_reduce_fusion.20 = (f32[12,512]{1,0:T(8,128)S(1)}, f32[12,512,1024]{2,1,0:T(8,128)}) fusion(f32[12,512]{1,0:T(8,128)S(1)} %copy-done.48, f32[12,512,1024]{2,1,0:T(8,128)} %get-tuple-element.1381, pred[512,1024]{1,0:T(8,128)(4,1)} %get-tuple-element.1378, bf16[512,12,64]{0,2,1:T(8,128)(2,1)} %bitcast.316, bf16[1024,12,64]{0,2,1:T(8,128)(2,1)} %bitcast.310), kind=kOutput, calls=%fused_computation.4.clone.1 | convolution fusion | flops 836757504 | bytes 53264384 | tf_op jit(solution)/shard_map/while/body/eval_jaxpr/qhd,khd->hqk/dot_general | solution.py:93
  1031.4 13.2 bitcast_reduce_fusion.6
  1048.3 18.6 %multiply_reduce_fusion.19 = (f32[12,512]{1,0:T(8,128)S(1)}, f32[12,512,1024]{2,1,0:T(8,128)}) fusion(f32[12,512]{1,0:T(8,128)S(1)} %copy-done.49, f32[12,512,1024]{2,1,0:T(8,128)} %get-tuple-element.1377, pred[512,1024]{1,0:T(8,128)(4,1)} %get-tuple-element.1373, bf16[512,12,64]{0,2,1:T(8,128)(2,1)} %bitcast.315, bf16[1024,12,64]{0,2,1:T(8,128)(2,1)} %bitcast.311), kind=kOutput, calls=%fused_computation.1.clone.1 | convolution fusion | flops 836757504 | bytes 53264384 | tf_op jit(solution)/shard_map/while/body/eval_jaxpr/qhd,khd->hqk/dot_general | solution.py:93
  1067.1 23.9 %multiply_convert_fusion.14 = bf16[12,512,1024]{2,1,0:T(8,128)(2,1)} fusion(f32[12,512,1024]{2,1,0:T(8,128)} %get-tuple-element.1399, f32[12,512]{1,0:T(8,128)S(1)} %get-tuple-element.1400, f32[12,512]{1,0:T(8,128)S(1)} %copy-done.48, f32[12,512,1024]{2,1,0:T(8,128)} %get-tuple-element.1381, pred[512,1024]{1,0:T(8,128)(4,1)} %get-tuple-element.1378), kind=kLoop, calls=%fused_computation.3.clone.1 | loop fusion | flops 37748736 | bytes 63488000 | tf_op jit(solution)/shard_map/while/body/eval_jaxpr/convert_element_type | solution.py:104
  1095.3 15.9 %multiply_convert_fusion.13 = bf16[12,512,1024]{2,1,0:T(8,128)(2,1)} fusion(f32[12,512,1024]{2,1,0:T(8,128)} %get-tuple-element.1396, f32[12,512]{1,0:T(8,128)S(1)} %get-tuple-element.1397, f32[12,512]{1,0:T(8,128)S(1)} %copy-done.49, f32[12,512,1024]{2,1,0:T(8,128)S(1)} %bitcast.299, pred[512,1024]{1,0:T(8,128)(4,1)} %get-tuple-element.1373), kind=kLoop, calls=%fused_computation.clone.1 | loop fusion | flops 37748736 | bytes 63488000 | tf_op jit(solution)/shard_map/while/body/eval_jaxpr/convert_element_type | solution.py:104
  1111.2 7.3 fusion.262
  1125.9 9.2 bitcast_reduce_fusion.8
  1135.1 9.2 bitcast_reduce_fusion.7
  1147.7 9.8 convolution_convert_fusion.21
  1169.4 15.8 %all-reduce.36 = (bf16[768]{0:T(1024)(128)(2,1)S(1)}, bf16[768]{0:T(1024)(128)(2,1)S(1)}, bf16[768]{0:T(1024)(128)(2,1)S(1)}, bf16[768]{0:T(1024)(128)(2,1)S(1)}...) all-reduce(bf16[768]{0:T(1024)(128)(2,1)S(1)} %get-tuple-element.14, ...), channel_id=3, replica_groups=mesh['rep'=8,'shard'=4] {'shard'}, use_global_device_ids=true, to_apply=%region_18.18.clone | all-reduce | flops 9984 | bytes 39936 | tf_op jit(solution)/shard_map/while
  1185.2 9.7 fusion.269
  1194.9 11.0 add_bitcast_fusion.2
  1215.0 63.1 %fusion.267 = bf16[512,768]{1,0:T(8,128)(2,1)} fusion(bf16[2000,768]{1,0:T(8,128)(2,1)S(1)} %multiply_convert_fusion.16), kind=kCustom, calls=%all-reduce-scatter.clone.1 | all-reduce-scatter fusion | flops 1572865 | bytes 3858944 | tf_op jit(solution)/shard_map/while
  1305.4 17.8 %reduce-scatter.19.cloned.1.call-done = bf16[768,768]{1,0:T(8,128)(2,1)} async-done(((bf16[3072,768]{1,0:T(8,128)(2,1)}), bf16[768,768]{1,0:T(8,128)(2,1)}) %reduce-scatter.19.cloned.1.call-update) | async-done | bytes 1179664 | tf_op jit(solution)/shard_map/while/body/eval_jaxpr/reduce_scatter | solution.py:323
  1341.3 17.5 %all-reduce.29 = (bf16[192]{0:T(256)(128)(2,1)S(1)}, bf16[192]{0:T(256)(128)(2,1)S(1)}, bf16[192]{0:T(256)(128)(2,1)S(1)}, bf16[192]{0:T(256)(128)(2,1)S(1)}, bf...) all-reduce(bf16[192]{0:T(256)(128)(2,1)S(1)} %convert_element_type., ...), channel_id=1, replica_groups=mesh['rep'=8,'shard'=4] {'rep'}, use_global_device_ids=true, to_apply=%region_44.45 | all-reduce | flops 2304 | bytes 9216 | tf_op jit(solution)/shard_map/psum | solution.py:338
  1363.9 78.5 %all-reduce.39.cloned.1.call-done = (bf16[500,768]{1,0:T(8,128)(2,1)}, bf16[192,768]{1,0:T(8,128)(2,1)}, bf16[192,768]{1,0:T(8,128)(2,1)}, bf16[192,768]{1,0:T(8...) async-done(((bf16[500,768]{1,0:T(8,128)(2,1)}, bf16[192,768]{1,0:T(8,128)(2,1)}, bf16[192,768]{1,0:T(8,128)(2,1)}, ...) | async-done | bytes 4306960 | tf_op jit(solution)/shard_map/psum | solution.py:337
  (771 shorter events, 310.1 us)
Async XLA Ops:
  8.8 28.1 %copy-start.75 = (bf16[768]{0:T(1024)(128)(2,1)S(1)}, bf16[768]{0:T(1024)(128)(2,1)}, u32[]{:S(2)}) copy-start(bf16[768]{0:T(1024)(128)(2,1)} %get-tuple-element.1571) | copy-start | bytes 4612 | tf_op jit(solution)/shard_map/while
  8.8 28.1 %copy-start.65 = (s32[2,1024]{1,0:T(2,128)S(1)}, s32[2,1024]{1,0:T(2,128)}, u32[]{:S(2)}) copy-start(s32[2,1024]{1,0:T(2,128)} %get-tuple-element.1562) | copy-start | bytes 24580 | tf_op jit(solution)/shard_map/while
  8.9 52.6 %all-gather.20.cloned.1.call-start = ((), (), s32[]{:S(2)}) async-start(), calls=%async_computation.9 | async-start | bytes 3870720 | tf_op jit(solution)/shard_map/while/body/eval_jaxpr/all_gather | solution.py:187
  9.6 78.4 %all-gather.24.cloned.1.call-start = ((), (), s32[]{:S(2)}) async-start(), calls=%async_computation.11 | async-start | bytes 1474560 | tf_op jit(solution)/shard_map/while/body/eval_jaxpr/all_gather | solution.py:190
  10.3 107.4 %all-gather.26.cloned.1.call-start = ((), (), s32[]{:S(2)}) async-start(), calls=%async_computation.12 | async-start | bytes 1474560 | tf_op jit(solution)/shard_map/while/body/eval_jaxpr/all_gather | solution.py:192
  11.1 136.2 %all-gather.22.cloned.1.call-start = ((), (), s32[]{:S(2)}) async-start(), calls=%async_computation.10 | async-start | bytes 1474560 | tf_op jit(solution)/shard_map/while/body/eval_jaxpr/all_gather | solution.py:193
  11.7 189.5 %all-gather.18.cloned.1.call-start = ((), (), s32[]{:S(2)}) async-start(), calls=%async_computation.8 | async-start | bytes 1474560 | tf_op jit(solution)/shard_map/while/body/eval_jaxpr/all_gather | solution.py:195
  12.2 223.6 %all-gather.16.cloned.1.call-start = ((), (), s32[]{:S(2)}) async-start(), calls=%async_computation.7 | async-start | bytes 5898240 | tf_op jit(solution)/shard_map/while/body/eval_jaxpr/all_gather | solution.py:199
  12.8 282.1 %all-gather.28.cloned.1.call-start = ((), (), s32[]{:S(2)}) async-start(), calls=%async_computation.13 | async-start | bytes 5898240 | tf_op jit(solution)/shard_map/while/body/eval_jaxpr/all_gather | solution.py:237
  13.6 622.4 %reduce-scatter.15.cloned.1.call-start = ((), (), s32[]{:S(2)}) async-start(), calls=%async_computation.17 | async-start | bytes 1474560 | tf_op jit(solution)/shard_map/while/body/eval_jaxpr/reduce_scatter | solution.py:305
  37.6 30.5 %copy-start.54 = (f32[768]{0:T(1024)}, f32[768]{0:T(1024)S(1)}, u32[]{:S(2)}) copy-start(f32[768]{0:T(1024)S(1)} %convert_element_type.808) | copy-start | bytes 9220 | tf_op jit(solution)/shard_map/while
  54.5 146.7 %copy-start.1 = (f32[1,1024,768]{1,2,0:T(8,128)}, f32[1,1024,768]{1,2,0:T(8,128)S(1)}, u32[]{:S(2)}) copy-start(f32[1,1024,768]{1,2,0:T(8,128)S(1)} %copy.83) | copy-start | bytes 9437188 | tf_op jit(solution)/shard_map/while
  65.5 135.7 %copy-start.50 = (f32[768]{0:T(1024)}, f32[768]{0:T(1024)S(1)}, u32[]{:S(2)}) copy-start(f32[768]{0:T(1024)S(1)} %convert_reduce_fusion.4) | copy-start | bytes 9220 | tf_op jit(solution)/shard_map/while
  175.0 16.6 %copy-start = (f32[12,512,1024]{2,1,0:T(8,128)S(1)}, f32[12,512,1024]{2,1,0:T(8,128)}, u32[]{:S(2)}) copy-start(f32[12,512,1024]{2,1,0:T(8,128)} %get-tuple-element.1377) | copy-start | bytes 75497472 | tf_op jit(solution)/shard_map/while
  204.7 31.1 %copy-start.58 = (f32[768]{0:T(1024)S(1)}, f32[768]{0:T(1024)}, u32[]{:S(2)}) copy-start(f32[768]{0:T(1024)} %convert_element_type.812) | copy-start | bytes 9220 | tf_op jit(solution)/shard_map/while
  204.7 31.1 %copy-start.64 = (f32[4,1,768]{2,1,0:T(1,128)S(1)}, f32[4,1,768]{2,1,0:T(1,128)}, u32[]{:S(2)}) copy-start(f32[4,1,768]{2,1,0:T(1,128)} %convert_element_type.805) | copy-start | bytes 36868 | tf_op jit(solution)/shard_map/while
  204.7 31.1 %copy-start.71 = (f32[768]{0:T(1024)S(1)}, f32[768]{0:T(1024)}, u32[]{:S(2)}) copy-start(f32[768]{0:T(1024)} %convert_element_type.811) | copy-start | bytes 9220 | tf_op jit(solution)/shard_map/while
  235.8 59.1 %copy-start.16 = (f32[1,1024,768]{1,2,0:T(8,128)S(1)}, f32[1,1024,768]{1,2,0:T(8,128)}, u32[]{:S(2)}) copy-start(f32[1,1024,768]{1,2,0:T(8,128)} %copy.84) | copy-start | bytes 9437188 | tf_op jit(solution)/shard_map/while
  337.0 300.9 %reduce-scatter.13.cloned.1.call-start = ((), (), s32[]{:S(2)}) async-start(), calls=%async_computation.16 | async-start | bytes 1474560 | tf_op jit(solution)/shard_map/while/body/eval_jaxpr/reduce_scatter | solution.py:299
  374.0 14.4 copy-start.37
  409.5 230.4 %reduce-scatter.11.cloned.1.call-start = ((), (), s32[]{:S(2)}) async-start(), calls=%async_computation.15 | async-start | bytes 1474560 | tf_op jit(solution)/shard_map/while/body/eval_jaxpr/reduce_scatter | solution.py:296
  409.6 23.9 %slice-start = ((s8[25165824]{0:T(1024)(128)(4,1)}), s8[4194304]{0:T(1024)(128)(4,1)S(1)}, s32[]{:S(2)}) async-start(s8[25165824]{0:T(1024)(128)(4,1)} %bitcast.298), calls=%async_computation.20 | async-start | bytes 8388608 | tf_op jit(solution)/shard_map/while
  409.6 23.9 %slice-start.1 = ((s8[25165824]{0:T(1024)(128)(4,1)}), s8[4194304]{0:T(1024)(128)(4,1)S(1)}, s32[]{:S(2)}) async-start(s8[25165824]{0:T(1024)(128)(4,1)} %bitcast.298), calls=%async_computation.21 | async-start | bytes 8388608 | tf_op jit(solution)/shard_map/while
  409.6 24.7 %slice-start.2 = ((s8[25165824]{0:T(1024)(128)(4,1)}), s8[4194304]{0:T(1024)(128)(4,1)S(1)}, s32[]{:S(2)}) async-start(s8[25165824]{0:T(1024)(128)(4,1)} %bitcast.298), calls=%async_computation.22 | async-start | bytes 8388608 | tf_op jit(solution)/shard_map/while
  409.6 25.9 %slice-start.3 = ((s8[25165824]{0:T(1024)(128)(4,1)}), s8[4194304]{0:T(1024)(128)(4,1)S(1)}, s32[]{:S(2)}) async-start(s8[25165824]{0:T(1024)(128)(4,1)} %bitcast.298), calls=%async_computation.23 | async-start | bytes 8388608 | tf_op jit(solution)/shard_map/while
  409.6 27.1 %slice-start.4 = ((s8[25165824]{0:T(1024)(128)(4,1)}), s8[4194304]{0:T(1024)(128)(4,1)S(1)}, s32[]{:S(2)}) async-start(s8[25165824]{0:T(1024)(128)(4,1)} %bitcast.298), calls=%async_computation.24 | async-start | bytes 8388608 | tf_op jit(solution)/shard_map/while
  409.6 28.3 %slice-start.5 = ((s8[25165824]{0:T(1024)(128)(4,1)}), s8[4194304]{0:T(1024)(128)(4,1)S(1)}, s32[]{:S(2)}) async-start(s8[25165824]{0:T(1024)(128)(4,1)} %bitcast.298), calls=%async_computation.25 | async-start | bytes 8388608 | tf_op jit(solution)/shard_map/while
  468.2 172.9 %reduce-scatter.9.cloned.1.call-start = ((), (), s32[]{:S(2)}) async-start(), calls=%async_computation.14 | async-start | bytes 1474560 | tf_op jit(solution)/shard_map/while/body/eval_jaxpr/reduce_scatter | solution.py:290
  490.2 153.5 %reduce-scatter.17.cloned.1.call-start = ((), (), s32[]{:S(2)}) async-start(), calls=%async_computation.18 | async-start | bytes 5898240 | tf_op jit(solution)/shard_map/while/body/eval_jaxpr/reduce_scatter | solution.py:317
  500.2 165.5 %reduce-scatter.19.cloned.1.call-start = ((), (), s32[]{:S(2)}) async-start(), calls=%async_computation.19 | async-start | bytes 5898240 | tf_op jit(solution)/shard_map/while/body/eval_jaxpr/reduce_scatter | solution.py:323
  621.3 11.9 collective-permute-start
  643.7 21.9 %copy-start.26 = (f32[768,768]{1,0:T(8,128)S(1)}, f32[768,768]{1,0:T(8,128)}, u32[]{:S(2)}) copy-start(f32[768,768]{1,0:T(8,128)} %get-tuple-element.1498) | copy-start | bytes 7077892 | tf_op jit(solution)/shard_map/while
  669.6 25.2 %copy-start.75 = (bf16[768]{0:T(1024)(128)(2,1)S(1)}, bf16[768]{0:T(1024)(128)(2,1)}, u32[]{:S(2)}) copy-start(bf16[768]{0:T(1024)(128)(2,1)} %get-tuple-element.1571) | copy-start | bytes 4612 | tf_op jit(solution)/shard_map/while
  669.6 25.2 %copy-start.65 = (s32[2,1024]{1,0:T(2,128)S(1)}, s32[2,1024]{1,0:T(2,128)}, u32[]{:S(2)}) copy-start(s32[2,1024]{1,0:T(2,128)} %get-tuple-element.1562) | copy-start | bytes 24580 | tf_op jit(solution)/shard_map/while
  669.6 50.6 %all-gather.20.cloned.1.call-start = ((), (), s32[]{:S(2)}) async-start(), calls=%async_computation.9 | async-start | bytes 3870720 | tf_op jit(solution)/shard_map/while/body/eval_jaxpr/all_gather | solution.py:187
  670.2 75.4 %all-gather.24.cloned.1.call-start = ((), (), s32[]{:S(2)}) async-start(), calls=%async_computation.11 | async-start | bytes 1474560 | tf_op jit(solution)/shard_map/while/body/eval_jaxpr/all_gather | solution.py:190
  670.8 104.4 %all-gather.26.cloned.1.call-start = ((), (), s32[]{:S(2)}) async-start(), calls=%async_computation.12 | async-start | bytes 1474560 | tf_op jit(solution)/shard_map/while/body/eval_jaxpr/all_gather | solution.py:192
  671.3 133.4 %all-gather.22.cloned.1.call-start = ((), (), s32[]{:S(2)}) async-start(), calls=%async_computation.10 | async-start | bytes 1474560 | tf_op jit(solution)/shard_map/while/body/eval_jaxpr/all_gather | solution.py:193
  671.9 186.7 %all-gather.18.cloned.1.call-start = ((), (), s32[]{:S(2)}) async-start(), calls=%async_computation.8 | async-start | bytes 1474560 | tf_op jit(solution)/shard_map/while/body/eval_jaxpr/all_gather | solution.py:195
  672.5 220.9 %all-gather.16.cloned.1.call-start = ((), (), s32[]{:S(2)}) async-start(), calls=%async_computation.7 | async-start | bytes 5898240 | tf_op jit(solution)/shard_map/while/body/eval_jaxpr/all_gather | solution.py:199
  673.3 279.1 %all-gather.28.cloned.1.call-start = ((), (), s32[]{:S(2)}) async-start(), calls=%async_computation.13 | async-start | bytes 5898240 | tf_op jit(solution)/shard_map/while/body/eval_jaxpr/all_gather | solution.py:237
  673.9 619.5 %reduce-scatter.15.cloned.1.call-start = ((), (), s32[]{:S(2)}) async-start(), calls=%async_computation.17 | async-start | bytes 1474560 | tf_op jit(solution)/shard_map/while/body/eval_jaxpr/reduce_scatter | solution.py:305
  695.5 31.4 %copy-start.54 = (f32[768]{0:T(1024)}, f32[768]{0:T(1024)S(1)}, u32[]{:S(2)}) copy-start(f32[768]{0:T(1024)S(1)} %convert_element_type.808) | copy-start | bytes 9220 | tf_op jit(solution)/shard_map/while
  713.2 145.4 %copy-start.1 = (f32[1,1024,768]{1,2,0:T(8,128)}, f32[1,1024,768]{1,2,0:T(8,128)S(1)}, u32[]{:S(2)}) copy-start(f32[1,1024,768]{1,2,0:T(8,128)S(1)} %copy.83) | copy-start | bytes 9437188 | tf_op jit(solution)/shard_map/while
  724.2 134.4 %copy-start.50 = (f32[768]{0:T(1024)}, f32[768]{0:T(1024)S(1)}, u32[]{:S(2)}) copy-start(f32[768]{0:T(1024)S(1)} %convert_reduce_fusion.4) | copy-start | bytes 9220 | tf_op jit(solution)/shard_map/while
  832.4 16.6 %copy-start = (f32[12,512,1024]{2,1,0:T(8,128)S(1)}, f32[12,512,1024]{2,1,0:T(8,128)}, u32[]{:S(2)}) copy-start(f32[12,512,1024]{2,1,0:T(8,128)} %get-tuple-element.1377) | copy-start | bytes 75497472 | tf_op jit(solution)/shard_map/while
  862.1 31.3 %copy-start.58 = (f32[768]{0:T(1024)S(1)}, f32[768]{0:T(1024)}, u32[]{:S(2)}) copy-start(f32[768]{0:T(1024)} %convert_element_type.812) | copy-start | bytes 9220 | tf_op jit(solution)/shard_map/while
  862.2 31.3 %copy-start.64 = (f32[4,1,768]{2,1,0:T(1,128)S(1)}, f32[4,1,768]{2,1,0:T(1,128)}, u32[]{:S(2)}) copy-start(f32[4,1,768]{2,1,0:T(1,128)} %convert_element_type.805) | copy-start | bytes 36868 | tf_op jit(solution)/shard_map/while
  862.2 31.3 %copy-start.71 = (f32[768]{0:T(1024)S(1)}, f32[768]{0:T(1024)}, u32[]{:S(2)}) copy-start(f32[768]{0:T(1024)} %convert_element_type.811) | copy-start | bytes 9220 | tf_op jit(solution)/shard_map/while
  893.4 58.9 %copy-start.16 = (f32[1,1024,768]{1,2,0:T(8,128)S(1)}, f32[1,1024,768]{1,2,0:T(8,128)}, u32[]{:S(2)}) copy-start(f32[1,1024,768]{1,2,0:T(8,128)} %copy.84) | copy-start | bytes 9437188 | tf_op jit(solution)/shard_map/while
  994.4 300.9 %reduce-scatter.13.cloned.1.call-start = ((), (), s32[]{:S(2)}) async-start(), calls=%async_computation.16 | async-start | bytes 1474560 | tf_op jit(solution)/shard_map/while/body/eval_jaxpr/reduce_scatter | solution.py:299
  1066.9 230.5 %reduce-scatter.11.cloned.1.call-start = ((), (), s32[]{:S(2)}) async-start(), calls=%async_computation.15 | async-start | bytes 1474560 | tf_op jit(solution)/shard_map/while/body/eval_jaxpr/reduce_scatter | solution.py:296
  1067.0 23.9 %slice-start = ((s8[25165824]{0:T(1024)(128)(4,1)}), s8[4194304]{0:T(1024)(128)(4,1)S(1)}, s32[]{:S(2)}) async-start(s8[25165824]{0:T(1024)(128)(4,1)} %bitcast.298), calls=%async_computation.20 | async-start | bytes 8388608 | tf_op jit(solution)/shard_map/while
  1067.0 23.9 %slice-start.1 = ((s8[25165824]{0:T(1024)(128)(4,1)}), s8[4194304]{0:T(1024)(128)(4,1)S(1)}, s32[]{:S(2)}) async-start(s8[25165824]{0:T(1024)(128)(4,1)} %bitcast.298), calls=%async_computation.21 | async-start | bytes 8388608 | tf_op jit(solution)/shard_map/while
  1067.0 24.7 %slice-start.2 = ((s8[25165824]{0:T(1024)(128)(4,1)}), s8[4194304]{0:T(1024)(128)(4,1)S(1)}, s32[]{:S(2)}) async-start(s8[25165824]{0:T(1024)(128)(4,1)} %bitcast.298), calls=%async_computation.22 | async-start | bytes 8388608 | tf_op jit(solution)/shard_map/while
  1067.0 25.9 %slice-start.3 = ((s8[25165824]{0:T(1024)(128)(4,1)}), s8[4194304]{0:T(1024)(128)(4,1)S(1)}, s32[]{:S(2)}) async-start(s8[25165824]{0:T(1024)(128)(4,1)} %bitcast.298), calls=%async_computation.23 | async-start | bytes 8388608 | tf_op jit(solution)/shard_map/while
  1067.0 27.1 %slice-start.4 = ((s8[25165824]{0:T(1024)(128)(4,1)}), s8[4194304]{0:T(1024)(128)(4,1)S(1)}, s32[]{:S(2)}) async-start(s8[25165824]{0:T(1024)(128)(4,1)} %bitcast.298), calls=%async_computation.24 | async-start | bytes 8388608 | tf_op jit(solution)/shard_map/while
  1067.0 28.3 %slice-start.5 = ((s8[25165824]{0:T(1024)(128)(4,1)}), s8[4194304]{0:T(1024)(128)(4,1)S(1)}, s32[]{:S(2)}) async-start(s8[25165824]{0:T(1024)(128)(4,1)} %bitcast.298), calls=%async_computation.25 | async-start | bytes 8388608 | tf_op jit(solution)/shard_map/while
  1125.7 173.0 %reduce-scatter.9.cloned.1.call-start = ((), (), s32[]{:S(2)}) async-start(), calls=%async_computation.14 | async-start | bytes 1474560 | tf_op jit(solution)/shard_map/while/body/eval_jaxpr/reduce_scatter | solution.py:290
  1147.7 153.8 %reduce-scatter.17.cloned.1.call-start = ((), (), s32[]{:S(2)}) async-start(), calls=%async_computation.18 | async-start | bytes 5898240 | tf_op jit(solution)/shard_map/while/body/eval_jaxpr/reduce_scatter | solution.py:317
  1157.6 165.5 %reduce-scatter.19.cloned.1.call-start = ((), (), s32[]{:S(2)}) async-start(), calls=%async_computation.19 | async-start | bytes 5898240 | tf_op jit(solution)/shard_map/while/body/eval_jaxpr/reduce_scatter | solution.py:323
  1278.9 11.7 collective-permute-start
  1301.5 21.7 %copy-start.26 = (f32[768,768]{1,0:T(8,128)S(1)}, f32[768,768]{1,0:T(8,128)}, u32[]{:S(2)}) copy-start(f32[768,768]{1,0:T(8,128)} %get-tuple-element.1498) | copy-start | bytes 7077892 | tf_op jit(solution)/shard_map/while
  1328.7 113.7 %all-reduce.39.cloned.1.call-start = ((), (), s32[]{:S(2)}) async-start(), calls=%async_computation.6 | async-start | bytes 8626176 | tf_op jit(solution)/shard_map/psum | solution.py:337
  (189 other events, 840.4 us)
Sparse Core Ops, SparseCore 0:
  11.7 46.4 all-gather.19
  60.2 27.7 all-gather.23
  90.0 27.7 all-gather.25
  119.6 27.7 all-gather.21
  149.1 27.7 all-gather.17
  178.7 57.0 all-gather.15
  237.8 57.0 all-gather.27
  337.1 28.5 reduce-scatter.14
  409.6 28.4 reduce-scatter.12
  468.3 28.6 reduce-scatter.10
  500.2 28.5 reduce-scatter.8
  531.9 69.5 reduce-scatter.16
  604.8 60.8 reduce-scatter.18
  672.1 43.7 all-gather.19
  717.8 27.7 all-gather.23
  747.4 27.7 all-gather.25
  777.0 27.7 all-gather.21
  806.6 27.7 all-gather.17
  836.3 57.0 all-gather.15
  895.3 57.0 all-gather.27
  994.5 28.5 reduce-scatter.14
  1067.1 28.4 reduce-scatter.12
  1125.8 28.6 reduce-scatter.10
  1157.5 28.5 reduce-scatter.8
  1189.4 69.5 reduce-scatter.16
  1262.1 60.9 reduce-scatter.18
Sparse Core Ops, SparseCore 1:
  1341.1 101.2 all-reduce.38
where the time goes:
time: 1470 us; the launch traced here: 1460 us
  matrix products  534 us (36%)
  waiting for transfers between devices  314 us (21%)
  other arithmetic  229 us (16%)
  blocking collectives  224 us (15%)
  local copies, waits for them, and re-layouts  123 us (8%)
  between operations  15.9 us (1%)
  loops' own time  15 us (1%)
    while x6, blocking collectives  191 us
    dot_general x12, matrix products, project(): return jnp.dot(left, right, preferred_element_type=jnp.float32)  125 us
    convert_element_type x4, other arithmetic, attend_backward(): grad_scores = (chance * (grad_chance - jnp.sum(chance * grad_chance, axis...  79.5 us
    psum x1, waiting for transfers between devices, local(): lax.psum(totals[0].astype(jnp.bfloat16), 'rep').astype(jnp.float32)  78.5 us
    dot_general x12, matrix products, project_back(): jnp.einsum('tb,ab->ta', left, right, preferred_element_type=jnp.float32)  76.1 us
    dot_general x4, matrix products, attend_backward(): jnp.einsum('qhd,khd->hqk', grad_rows, v_heads, preferred_element_type=jnp...  74.2 us
    while x462, local copies, waits for them, and re-layouts  60.6 us
    dot_general x12, matrix products, project_left(): jnp.einsum('ta,tb->ab', left, right, preferred_element_type=jnp.float32)  58.5 us
  transfers between devices with their start and end apart: 29, of which 13 were waited for; matrix products, arithmetic and copies ran while one was open for 59% of the time, Pallas kernels for 0%

commit v1 on v0

v1 whole, which is shorter than its diff:
```python
import functools
import math

import jax
import jax.numpy as jnp
from jax import lax
from jax.experimental import pallas as pl
from jax.experimental.pallas import tpu as pltpu
from jax.sharding import PartitionSpec as P

NEG=-1e30
L=1024; QB=256
BF=jnp.bfloat16; F32=jnp.float32
LOG2E=math.log2(math.e); LN2=math.log(2.0)
def nt(a,b): return lax.dot_general(a,b,(((1,),(1,)),((),())),preferred_element_type=F32)
def nn(a,b): return lax.dot_general(a,b,(((1,),(0,)),((),())),preferred_element_type=F32)
def tn(a,b): return lax.dot_general(a,b,(((0,),(0,)),((),())),preferred_element_type=F32)

def seg_features(seg):
    lane=jnp.arange(128)%64
    hit=(seg[:,None]==lane[None,:])
    fq=jnp.where((lane<4)[None]&hit,1.0,0.0).astype(BF)
    fk=jnp.where((lane<4)[None],jnp.where(hit,0.0,NEG),jnp.where(((lane>=4)&(lane<7))[None],1.0,0.0)).astype(BF)
    return fq,fk

def fwd_kernel(q_ref,k_ref,v_ref,fq_ref,fk_ref,o_ref,fx_ref,*,qb):
    lane=lax.broadcasted_iota(jnp.int32,(1,128),1)
    lo=lane<64
    ks=[];vs=[]
    k=k_ref[...];v=v_ref[...];fk=fk_ref[...]
    for h in (0,1):
        own=lo if h==0 else ~lo
        ks.append(jnp.where(own,k,fk))
        vs.append(jnp.where(own,v,jnp.where((lane&63)==0,1.0,0.0).astype(BF)))
    for b in range(L//qb):
        rows=pl.ds(b*qb,qb)
        q=q_ref[rows,:];fq=fq_ref[rows,:]
        accs=[];ls=[]
        for h in (0,1):
            own=lo if h==0 else ~lo
            s=nt(jnp.where(own,q,fq),ks[h])
            m=jnp.max(s,axis=1,keepdims=True)
            p=jnp.exp2(s-m).astype(BF)
            acc=nn(p,vs[h])
            l=acc[:,64:65] if h==0 else acc[:,0:1]
            accs.append(acc*(1.0/l))
            ls.append(-(m+jnp.log2(l)))
        o_ref[rows,:]=jnp.where(lo,accs[0],accs[1]).astype(BF)
        nl=jnp.where(lo,ls[1],ls[0])
        hi=nl.astype(BF).astype(F32)
        r1=nl-hi
        mid=r1.astype(BF).astype(F32)
        r2=r1-mid
        l6=lane&63
        fx_ref[rows,:]=jnp.where(l6==4,hi,jnp.where(l6==5,mid,jnp.where(l6==6,r2,fq.astype(F32)))).astype(BF)

def attn_fwd(q,k,v,fq,fk,nseq,npair,qb=256):
    T=nseq*L
    blk=pl.BlockSpec((L,128),lambda s,p:(s,p))
    fb=pl.BlockSpec((L,128),lambda s,p:(s,0))
    return pl.pallas_call(functools.partial(fwd_kernel,qb=qb),grid=(nseq,npair),
        in_specs=[blk,blk,blk,fb,fb],out_specs=[blk,blk],
        out_shape=[jax.ShapeDtypeStruct((T,npair*128),BF)]*2,
        compiler_params=pltpu.CompilerParams(dimension_semantics=("arbitrary","arbitrary")),
        name="attn_fwd")(q,k,v,fq,fk)

def bwd_kernel(q_ref,k_ref,v_ref,fx_ref,fk_ref,o_ref,do_ref,dq_ref,dk_ref,dv_ref,dqa,*,qb,mode,kb):
    lane=lax.broadcasted_iota(jnp.int32,(1,128),1)
    lo=lane<64; l6=lane&63
    zero=jnp.zeros((),BF)
    ones2=jnp.where(l6<2,1.0,0.0).astype(BF)
    k=k_ref[...];v=v_ref[...];fk=fk_ref[...]
    kx=[];vx=[];km=[]
    for h in (0,1):
        own=lo if h==0 else ~lo
        kx.append(jnp.where(own,k,fk)); vx.append(jnp.where(own,v,ones2)); km.append(jnp.where(own,k,zero))
    dv=jnp.zeros((L,128),F32); dk=jnp.zeros((L,128),F32)
    for b in range(L//qb):
        rows=pl.ds(b*qb,qb)
        q=q_ref[rows,:];fx=fx_ref[rows,:];do=do_ref[rows,:]
        prod=do.astype(F32)*o_ref[rows,:].astype(F32)
        d0=-jnp.sum(jnp.where(lo,prod,0.0),axis=1,keepdims=True)
        d1=-jnp.sum(jnp.where(lo,0.0,prod),axis=1,keepdims=True)
        nd=jnp.where(lo,d1,d0)
        hi=nd.astype(BF).astype(F32)
        fd=jnp.where(l6==0,hi,jnp.where(l6==1,nd-hi,0.0)).astype(BF)
        dq=jnp.zeros((qb,128),F32)
        for h in (0,1):
            own=lo if h==0 else ~lo
            qx=jnp.where(own,q,fx); dx=jnp.where(own,do,fd)
            qm=jnp.where(own,q,zero); dm=jnp.where(own,do,zero)
            st=nt(kx[h],qx)
            p=jnp.exp2(st)
            dpt=nt(vx[h],dx)
            pb=p.astype(BF)
            ds=(p*dpt).astype(BF)
            dv=dv+nn(pb,dm)
            dk=dk+nn(ds,qm)
            dq=dq+tn(ds,km[h])
        dq_ref[rows,:]=(dq*0.125).astype(BF)
    dv_ref[...]=dv.astype(BF)
    dk_ref[...]=(dk*LN2).astype(BF)

def attn_bwd(q,k,v,fx,fk,o,do,nseq,npair,qb=256,mode=0,kb=256):
    T=nseq*L
    blk=pl.BlockSpec((L,128),lambda s,p:(s,p))
    fb=pl.BlockSpec((L,128),lambda s,p:(s,0))
    return pl.pallas_call(functools.partial(bwd_kernel,qb=qb,mode=mode,kb=kb),grid=(nseq,npair),
        in_specs=[blk,blk,blk,blk,fb,blk,blk],out_specs=[blk]*3,
        out_shape=[jax.ShapeDtypeStruct((T,npair*128),BF)]*3,
        scratch_shapes=[pltpu.VMEM((L,128),F32)],
        compiler_params=pltpu.CompilerParams(dimension_semantics=("arbitrary","arbitrary")),
        name="attn_bwd")(q,k,v,fx,fk,o,do)

EPS=1e-5
D=768;FF=3072

def mid_kernel(tok_ref,row_ref,att_ref,cot_ref,ow_ref,up_ref,dn_ref,vec_ref,ub_ref,
               res_ref,gm_ref,ga_ref,dup_ref,ddn_ref,dow_ref,sv_ref,sub_ref,
               aup,adn,aow,*,tb,fc,erfmode):
    i=pl.program_id(0)
    n=pl.num_programs(0)
    @pl.when(i==0)
    def _():
        aup[...]=jnp.zeros_like(aup);adn[...]=jnp.zeros_like(adn);aow[...]=jnp.zeros_like(aow)
        sv_ref[...]=jnp.zeros_like(sv_ref);sub_ref[...]=jnp.zeros_like(sub_ref)
    ob=vec_ref[0:1,:];g2=vec_ref[1:2,:];b2=vec_ref[2:3,:];db=vec_ref[3:4,:]
    att=att_ref[...]
    mixed=tok_ref[...]+row_ref[0]+nn(att,ow_ref[...])+ob
    mean=jnp.mean(mixed,axis=1,keepdims=True)
    off=mixed-mean
    var=jnp.mean(off*off,axis=1,keepdims=True)
    r=lax.rsqrt(var+EPS)
    xhat=off*r
    n2=(xhat*g2+b2).astype(BF)
    n2t=n2.T
    cot=cot_ref[...]
    g=cot.astype(BF)
    gt=g.T
    res=mixed+db
    gn2=jnp.zeros((tb,D),F32)
    for j in range(FF//fc):
        cs=slice(j*fc,(j+1)*fc)
        pre=nn(n2,up_ref[:,cs])+ub_ref[:,cs]
        gact=nt(g,dn_ref[cs,:])
        if erfmode==0:
            phi=0.5+0.5*lax.erf(pre*(2**-0.5))
            pdf=jnp.exp2(pre*pre*(-0.5*LOG2E))*(1.0/math.sqrt(2*math.pi))
        else:
            z=jnp.abs(pre)
            e=jnp.exp2(pre*pre*(-0.5*LOG2E))
            t=1.0/(1.0+(0.3275911*2**-0.5)*z)
            poly=t*(0.5*0.254829592+t*(-0.5*0.284496736+t*(0.5*1.421413741+t*(-0.5*1.453152027+t*(0.5*1.061405429)))))
            tail=poly*e
            phi=jnp.where(pre>=0,1.0-tail,tail)
            pdf=e*(1.0/math.sqrt(2*math.pi))
        act=(pre*phi).astype(BF)
        gp=gact*(phi+pre*pdf)
        gpre=gp.astype(BF)
        sub_ref[:,cs]+=jnp.sum(gp.reshape(tb//8,8,fc),axis=0)
        res=res+nn(act,dn_ref[cs,:])
        gn2=gn2+nt(gpre,up_ref[:,cs])
        adn[:,cs]+=nn(gt,act)
        aup[:,cs]+=nn(n2t,gpre)
    res_ref[...]=res
    e=gn2*g2
    c1=jnp.mean(e,axis=1,keepdims=True)
    c2=jnp.mean(e*xhat,axis=1,keepdims=True)
    gm=cot+r*(e-c1-xhat*c2)
    gml=gm.astype(BF)
    gm_ref[...]=gml
    ga_ref[...]=nt(gml,ow_ref[...]).astype(BF)
    aow[...]+=tn(att,gml)
    def s8(x): return jnp.sum(x.reshape(tb//8,8,D),axis=0)
    sv_ref[0:8,:]+=s8(gm)
    sv_ref[8:16,:]+=s8(gn2*xhat)
    sv_ref[16:24,:]+=s8(gn2)
    sv_ref[24:32,:]+=s8(cot)
    @pl.when(i==n-1)
    def _():
        dow_ref[...]=aow[...].astype(BF)
        dup_ref[...]=aup[...].astype(BF)
        eye=(lax.broadcasted_iota(jnp.int32,(256,256),0)==lax.broadcasted_iota(jnp.int32,(256,256),1)).astype(BF)
        for c in range(FF//256):
            ddn_ref[c*256:(c+1)*256,:]=nt(eye,adn[:,c*256:(c+1)*256].astype(BF)).astype(BF)

def mid(tok,row,att,cot,ow,up,dn,vec,ub,tb=512,fc=512,erfmode=0):
    T=tok.shape[0]
    per=1024//tb
    blk=pl.BlockSpec((tb,D),lambda i:(i,0))
    def full(*s): return pl.BlockSpec(s,lambda i:(0,)*len(s),pipeline_mode=pl.Buffered(1))
    return pl.pallas_call(functools.partial(mid_kernel,tb=tb,fc=fc,erfmode=erfmode),grid=(T//tb,),
        in_specs=[blk,pl.BlockSpec((1,1,D),lambda i:(i//per,0,0)),blk,blk,full(D,D),full(D,FF),full(FF,D),full(8,D),full(1,FF)],
        out_specs=[blk,blk,blk,full(D,FF),full(FF,D),full(D,D),full(32,D),full(8,FF)],
        out_shape=[jax.ShapeDtypeStruct((T,D),F32),jax.ShapeDtypeStruct((T,D),BF),jax.ShapeDtypeStruct((T,D),BF),
            jax.ShapeDtypeStruct((D,FF),BF),jax.ShapeDtypeStruct((FF,D),BF),jax.ShapeDtypeStruct((D,D),BF),
            jax.ShapeDtypeStruct((32,D),F32),jax.ShapeDtypeStruct((8,FF),F32)],
        scratch_shapes=[pltpu.VMEM((D,FF),F32),pltpu.VMEM((D,FF),F32),pltpu.VMEM((D,D),F32)],
        compiler_params=pltpu.CompilerParams(dimension_semantics=("arbitrary",),vmem_limit_bytes=66*1024*1024-2**21),
        name="mid")(tok,row,att,cot,ow,up,dn,vec,ub)

EPS=1e-5
D=768
QS=0.125*LOG2E
def full(*s): return pl.BlockSpec(s,lambda i:(0,)*len(s),pipeline_mode=pl.Buffered(1))
def norm(x):
    mean=jnp.mean(x,axis=1,keepdims=True)
    off=x-mean
    var=jnp.mean(off*off,axis=1,keepdims=True)
    r=lax.rsqrt(var+EPS)
    return off*r,r
def qkv_kernel(tok_ref,row_ref,wq_ref,wk_ref,wv_ref,vec_ref,q_ref,k_ref,v_ref):
    xhat,_=norm(tok_ref[...]+row_ref[0])
    n1=(xhat*vec_ref[0:1,:]+vec_ref[1:2,:]).astype(BF)
    q_ref[...]=((nn(n1,wq_ref[...])+vec_ref[2:3,:])*QS).astype(BF)
    k_ref[...]=nn(n1,wk_ref[...]).astype(BF)
    v_ref[...]=(nn(n1,wv_ref[...])+vec_ref[3:4,:]).astype(BF)
def qkv(tok,row,wq,wk,wv,vec,tb=512):
    T=tok.shape[0];per=1024//tb
    blk=pl.BlockSpec((tb,D),lambda i:(i,0))
    return pl.pallas_call(qkv_kernel,grid=(T//tb,),
      in_specs=[blk,pl.BlockSpec((1,1,D),lambda i:(i//per,0,0)),full(D,D),full(D,D),full(D,D),full(8,D)],
      out_specs=[blk]*3,out_shape=[jax.ShapeDtypeStruct((T,D),BF)]*3,
      compiler_params=pltpu.CompilerParams(dimension_semantics=("arbitrary",)),name="qkv")(tok,row,wq,wk,wv,vec)

def last_kernel(tok_ref,row_ref,dq_ref,dk_ref,dv_ref,gm_ref,wq_ref,wk_ref,wv_ref,vec_ref,
                gt_ref,dwq_ref,dwk_ref,dwv_ref,sv_ref,ts_ref,aq,ak,av,*,tb,per):
    i=pl.program_id(0);n=pl.num_programs(0)
    @pl.when(i==0)
    def _():
        aq[...]=jnp.zeros_like(aq);ak[...]=jnp.zeros_like(ak);av[...]=jnp.zeros_like(av)
        sv_ref[...]=jnp.zeros_like(sv_ref)
    @pl.when(i%per==0)
    def _(): ts_ref[...]=jnp.zeros_like(ts_ref)
    g1=vec_ref[0:1,:]
    xhat,r=norm(tok_ref[...]+row_ref[0])
    n1t=(xhat*g1+vec_ref[1:2,:]).astype(BF).T
    dq=dq_ref[...];dk=dk_ref[...];dv=dv_ref[...]
    gn=nt(dq,wq_ref[...])+nt(dk,wk_ref[...])+nt(dv,wv_ref[...])
    aq[...]+=nn(n1t,dq);ak[...]+=nn(n1t,dk);av[...]+=nn(n1t,dv)
    e=gn*g1
    c1=jnp.mean(e,axis=1,keepdims=True)
    c2=jnp.mean(e*xhat,axis=1,keepdims=True)
    gt=gm_ref[...].astype(F32)+r*(e-c1-xhat*c2)
    gt_ref[...]=gt
    def s8(x): return jnp.sum(x.reshape(tb//8,8,D),axis=0)
    sv_ref[0:8,:]+=s8(gn*xhat)
    sv_ref[8:16,:]+=s8(gn)
    sv_ref[16:24,:]+=s8(dq.astype(F32))
    sv_ref[24:32,:]+=s8(dv.astype(F32))
    ts_ref[0]+=s8(gt)
    @pl.when(i==n-1)
    def _():
        dwq_ref[...]=aq[...].astype(BF);dwk_ref[...]=ak[...].astype(BF);dwv_ref[...]=av[...].astype(BF)
def last(tok,row,dq,dk,dv,gm,wq,wk,wv,vec,tb=256):
    T=tok.shape[0];per=1024//tb
    blk=pl.BlockSpec((tb,D),lambda i:(i,0))
    S=jax.ShapeDtypeStruct
    return pl.pallas_call(functools.partial(last_kernel,tb=tb,per=per),grid=(T//tb,),
      in_specs=[blk,pl.BlockSpec((1,1,D),lambda i:(i//per,0,0)),blk,blk,blk,blk,full(D,D),full(D,D),full(D,D),full(8,D)],
      out_specs=[blk,full(D,D),full(D,D),full(D,D),full(32,D),pl.BlockSpec((1,8,D),lambda i:(i//per,0,0))],
      out_shape=[S((T,D),F32),S((D,D),BF),S((D,D),BF),S((D,D),BF),S((32,D),F32),S((T//1024,8,D),F32)],
      scratch_shapes=[pltpu.VMEM((D,D),F32)]*3,
      compiler_params=pltpu.CompilerParams(dimension_semantics=("arbitrary",)),name="last")(tok,row,dq,dk,dv,gm,wq,wk,wv,vec)

def local(tokens,segments,time_steps,time_table,ln1_gain,ln1_bias,q_weight,q_bias,k_weight,v_weight,v_bias,o_weight,o_bias,ln2_gain,ln2_bias,up_weight,up_bias,down_weight,down_bias,cotangent):
    nseq=tokens.shape[0]
    T=nseq*L
    S=lax.axis_size("shard")
    me=lax.axis_index("shard")
    ag=lambda x: lax.all_gather(x,"shard",axis=0,tiled=True)
    small=jnp.concatenate([ln1_gain,ln1_bias,q_bias,v_bias,o_bias,ln2_gain,ln2_bias,down_bias,up_bias])
    w=ln1_gain.shape[0]
    steps=lax.all_gather(time_steps,"shard",axis=0,tiled=True)
    own=time_table.shape[0]
    idx=steps-me*own
    mine=(idx>=0)&(idx<own)
    rows=jnp.where(mine[:,None],time_table[jnp.clip(idx,0,own-1)],jnp.zeros((),BF))
    rows=lax.psum_scatter(rows,"shard",scatter_dimension=0,tiled=True).astype(F32).reshape(nseq,1,D)
    sm=lax.all_gather(small,"shard",axis=0,tiled=False)
    vecs=[sm[:,i*w:(i+1)*w].reshape(-1).astype(F32) for i in range(8)]
    ub=sm[:,8*w:].reshape(1,-1).astype(F32)
    g1,b1,qb,vb,ob,g2,b2,db=vecs
    z=jnp.zeros_like(g1)
    wq,wk,wv=ag(q_weight),ag(k_weight),ag(v_weight)
    ow,up,dn=ag(o_weight),ag(up_weight),ag(down_weight)
    tok=tokens.reshape(T,D)
    vec1=jnp.stack([g1,b1,qb,vb,z,z,z,z])
    vec2=jnp.stack([ob,g2,b2,db,z,z,z,z])
    fq,fk=seg_features(segments.reshape(T))
    q,k,v=qkv(tok,rows,wq,wk,wv,vec1)
    att,fx=attn_fwd(q,k,v,fq,fk,nseq,6,512)
    res,gm,ga,dup,ddn,dow,sv2,sub=mid(tok,rows,att,cotangent.reshape(T,D),ow,up,dn,vec2,ub,256,512)
    dq,dk,dv=attn_bwd(q,k,v,fx,fk,att,ga,nseq,6,256)
    gt,dwq,dwk,dwv,sv1,ts=last(tok,rows,dq,dk,dv,gm,wq,wk,wv,vec1)
    def red(x): return lax.psum(lax.psum_scatter(x,"shard",scatter_dimension=0,tiled=True),"rep").astype(F32)
    s2=sv2.reshape(4,8,D).sum(1);s1=sv1.reshape(4,8,D).sum(1)
    allv=jnp.concatenate([s1,s2]).reshape(-1,S,w).transpose(1,0,2).astype(BF)
    sums=lax.psum(lax.psum_scatter(allv,"shard",scatter_dimension=0,tiled=True),"rep").astype(F32).reshape(-1,w)
    subs=lax.psum(lax.psum_scatter(sub.sum(0).astype(BF),"shard",scatter_dimension=0,tiled=True),"rep").astype(F32)
    tt=lax.all_gather(ts.sum(1).astype(BF),("rep","shard"),axis=0,tiled=True)
    st=lax.all_gather(time_steps,("rep","shard"),axis=0,tiled=True)
    ids=me*own+jnp.arange(own)
    gtab=jnp.dot((ids[:,None]==st[None,:]).astype(BF),tt,preferred_element_type=F32)
    return (res.reshape(tokens.shape),gt.reshape(tokens.shape),gtab,sums[0],sums[1],red(dwq),sums[2],red(dwk),red(dwv),sums[3],red(dow),sums[4],sums[5],sums[6],red(dup),subs,red(ddn),sums[7])


def solution(mesh):
    b=("rep","shard")
    s=P("shard"); m=P("shard",None); t=P(b,None,None)
    return jax.shard_map(local,mesh=mesh,
        in_specs=(t,P(b,None),P(b),m,s,s,m,s,m,m,s,m,s,s,s,m,s,m,s,t),
        out_specs=(t,t,m,s,s,m,s,m,m,s,m,s,s,s,m,s,m,s),check_vma=False)
```

time: 1470 us -> 834 us (0.57)
  matrix products: 534 us -> 1.55 us
  Pallas kernels: 0 us -> 240 us
  other arithmetic: 229 us -> 11.3 us
  local copies, waits for them, and re-layouts: 123 us -> 7.72 us
  waiting for transfers between devices: 314 us -> 387 us
  blocking collectives: 224 us -> 168 us
  loops' own time: 15 us -> 0 us
    dot_general x60 -> x1, matrix products: 534 us -> 1.55 us  [local(): jnp.dot((ids[:, None] == st[None, :]).astype(BF), tt, preferred_element_t...]
    pallas_call x0 -> x5, Pallas kernels: none -> 240 us  [the longest x1 88.8 us: mid(): pl.pallas_call(functools.partial(mid_kernel, tb=tb, fc=fc, erfmode=erfmod...]
    reduce_scatter x12 -> x6, waiting for transfers between devices: 36.6 us -> 241 us  [red(): lax.psum_scatter(x, 'shard', scatter_dimension=0, tiled=True)]
    while x6 -> x0, blocking collectives: 191 us -> none
    convert_element_type x62 -> x10, other arithmetic: 123 us -> 11 us  [the longest x6 8.06 us: red(): lax.psum(lax.psum_scatter(x, 'shard', scatter_dimension=0, tiled=True), '...]
    unnamed x0 -> x4, blocking collectives: none -> 81.6 us
    psum x1, waiting for transfers between devices: 78.5 us -> 0.01 us  [red(): lax.psum(lax.psum_scatter(x, 'shard', scatter_dimension=0, tiled=True), '...]
    reduce_sum x20 -> x4, other arithmetic: 67.4 us -> 0.14 us  [the longest x1 0.04 us: local(): s2 = sv2.reshape(4, 8, D).sum(1)]
  transfers between devices with their start and end apart: 29 -> 13, of which waited for: 13 -> 10; matrix products, arithmetic and copies ran while one was open for 59% -> 1% of each run, Pallas kernels for 0% -> 7%
where the time goes in v1:
time: 834 us; the launch traced here: 833 us
  waiting for transfers between devices  387 us (46%)
  Pallas kernels  240 us (29%)
  blocking collectives  168 us (20%)
  between operations  16.2 us (2%)
  other arithmetic  11.3 us (1%)
    reduce_scatter x6, waiting for transfers between devices, red(): lax.psum_scatter(x, 'shard', scatter_dimension=0, tiled=True)  241 us
    all_gather x6, waiting for transfers between devices, local(): ag = lambda x: lax.all_gather(x, 'shard', axis=0, tiled=True)  139 us
    pallas_call x1, Pallas kernels, mid(): pl.pallas_call(functools.partial(mid_kernel, tb=tb, fc=fc, erfmode=erfmod...  88.8 us
    unnamed x4, blocking collectives  81.6 us
    pallas_call x1, Pallas kernels, attn_bwd(): pl.pallas_call(functools.partial(bwd_kernel, qb=qb, mode=mode, kb=kb), gr...  71.8 us
    all_gather x1, blocking collectives, local(): lax.all_gather(ts.sum(1).astype(BF), ('rep', 'shard'), axis=0, tiled=True)  64.3 us
    pallas_call x1, Pallas kernels, attn_fwd(): pl.pallas_call(functools.partial(fwd_kernel, qb=qb), grid=(nseq, npair),...  41.6 us
    pallas_call x1, Pallas kernels, last(): pl.pallas_call(functools.partial(last_kernel, tb=tb, per=per), grid=(T //...  24.9 us
  transfers between devices with their start and end apart: 13, of which 10 were waited for; matrix products, arithmetic and copies ran while one was open for 1% of the time, Pallas kernels for 7%

profile of v1, /device:TPU:0, one launch (start us, length us, event | category | flops | bytes accessed | tf_op | source)
XLA Modules:
  0.0 833.1 jit_solution(4354225948656264051)
XLA Ops:
  7.4 0.7 all-gather.10.cloned.1.call-update
  8.1 0.7 all-gather.12.cloned.1.call-update
  8.8 0.7 all-gather.14.cloned.1.call-update
  9.6 0.5 all-gather.16.cloned.1.call-update
  10.2 0.5 all-gather.18.cloned.1.call-update
  10.7 0.5 all-gather.20.cloned.1.call-update
  11.3 0.6 fusion.7
  12.6 0.2 dynamic-update-slice
  12.8 8.8 %all-reduce = s32[8]{0:T(128)S(1)} all-reduce(s32[8]{0:T(128)S(1)} %dynamic-update-slice), channel_id=1, replica_groups=mesh['rep'=8,'shard'=4] {'shard'}, use_global_device_ids=true, to_apply=%add | all-reduce | flops 8 | bytes 64
  21.7 0.1 concatenate.7
  21.8 8.2 all-gather.1
  30.0 0.1 slice_convert_fusion
  30.1 0.1 reshape.233
  30.2 0.1 reshape.234
  30.3 0.1 reshape.235
  30.4 0.1 reshape.236
  30.5 1.8 gather_fusion
  33.0 15.2 %all-reduce.2 = bf16[8,768]{1,0:T(8,128)(2,1)S(1)} all-reduce(bf16[8,768]{1,0:T(8,128)(2,1)S(1)} %broadcast_select_fusion), channel_id=3, replica_groups=mesh['rep'=8,'shard'=4] {'shard'}, use_global_device_ids=true, to_apply=%region_0.1.clone | all-reduce | flops 6144 | bytes 24576
  48.2 0.6 reshape.232.row_ref
  48.8 0.1 reshape.237
  48.9 0.1 reshape.238
  49.0 0.1 reshape.239
  49.1 0.1 reshape.240
  49.2 0.6 copy.41
  49.8 0.6 stack.4.vec_ref
  50.4 0.6 stack.5.vec_ref
  51.1 1.1 select_convert_fusion.fq_ref
  52.2 1.1 fusion.1.fk_ref
  53.3 17.1 %all-gather.12.cloned.1.call-done.wk_ref = bf16[768,768]{1,0:T(8,128)(2,1)} async-done(((bf16[192,768]{1,0:T(8,128)(2,1)}), bf16[768,768]{1,0:T(8,128)(2,1)}) %all-gather.12.cloned.1.call-update) | async-done | bytes 1179664 | tf_op jit(solution)/shard_map/all_gather | solution.py:271
  70.4 29.6 %all-gather.14.cloned.1.call-done.wv_ref = bf16[768,768]{1,0:T(8,128)(2,1)} async-done(((bf16[192,768]{1,0:T(8,128)(2,1)}), bf16[768,768]{1,0:T(8,128)(2,1)}) %all-gather.14.cloned.1.call-update) | async-done | bytes 1179664 | tf_op jit(solution)/shard_map/all_gather | solution.py:271
  100.0 12.8 %qkv.1 = (bf16[2048,768]{1,0:T(8,128)(2,1)}, bf16[2048,768]{1,0:T(8,128)(2,1)}, bf16[2048,768]{1,0:T(8,128)(2,1)}) custom-call(f32[2048,768]{1,0:T(8,128)} %bitcast.34, f32[2,1,768]{2,1,0:T(1,128)} %reshape.232.row_ref, bf16[768,768]{1,0:T(8,128)(2,1)} %all-gather.10.cloned.1.call-done.wq_ref, bf16[768,768]{1,0:T(8,128)(2,1)} %all-gather.12.cloned.1.call-done.wk_ref, ...), custom_call_target="tpu_custom_call" | custom-call | tf_op jit(solution)/shard_map/qkv/pallas_call | solution.py:221
  112.9 41.6 %attn_fwd.1 = (bf16[2048,768]{1,0:T(8,128)(2,1)}, bf16[2048,768]{1,0:T(8,128)(2,1)}) custom-call(bf16[2048,768]{1,0:T(8,128)(2,1)} %get-tuple-element.40.q_ref, bf16[2048,768]{1,0:T(8,128)(2,1)} %get-tuple-element.41.k_ref, bf16[2048,768]{1,0:T(8,128)(2,1)} %get-tuple-element.42.v_ref, bf16[2048,128]{1,0:T(8,128)(2,1)} %select_convert_fusion.fq_ref, ...), custom_call_target="tpu_custom_call" | custom-call | tf_op jit(solution)/shard_map/attn_fwd/pallas_call | solution.py:61
  154.5 33.8 %all-gather.18.cloned.1.call-done.up_ref = bf16[768,3072]{1,0:T(8,128)(2,1)} async-done(((bf16[192,3072]{1,0:T(8,128)(2,1)}), bf16[768,3072]{1,0:T(8,128)(2,1)}) %all-gather.18.cloned.1.call-update) | async-done | bytes 4718608 | tf_op jit(solution)/shard_map/all_gather | solution.py:271
  188.3 58.8 %all-gather.20.cloned.1.call-done.dn_ref = bf16[3072,768]{1,0:T(8,128)(2,1)} async-done(((bf16[768,768]{1,0:T(8,128)(2,1)}), bf16[3072,768]{1,0:T(8,128)(2,1)}) %all-gather.20.cloned.1.call-update) | async-done | bytes 4718608 | tf_op jit(solution)/shard_map/all_gather | solution.py:271
  247.1 88.8 %mid.1 = (f32[2048,768]{1,0:T(8,128)}, bf16[2048,768]{1,0:T(8,128)(2,1)}, bf16[2048,768]{1,0:T(8,128)(2,1)}, bf16[768,3072]{1,0:T(8,128)(2,1)}, bf16[3072,768]{1...) custom-call(f32[2048,768]{1,0:T(8,128)} %bitcast.35, ...), custom_call_target="tpu_custom_call" | custom-call | tf_op jit(solution)/shard_map/mid/pallas_call | solution.py:192
  335.9 71.8 %attn_bwd.1 = (bf16[2048,768]{1,0:T(8,128)(2,1)}, bf16[2048,768]{1,0:T(8,128)(2,1)}, bf16[2048,768]{1,0:T(8,128)(2,1)}) custom-call(bf16[2048,768]{1,0:T(8,128)(2,1)} %get-tuple-element.40.q_ref, bf16[2048,768]{1,0:T(8,128)(2,1)} %get-tuple-element.41.k_ref, bf16[2048,768]{1,0:T(8,128)(2,1)} %get-tuple-element.42.v_ref, ...), custom_call_target="tpu_custom_call" | custom-call | tf_op jit(solution)/shard_map/attn_bwd/pallas_call | solution.py:108
  407.7 24.9 %last.1 = (f32[2048,768]{1,0:T(8,128)}, bf16[768,768]{1,0:T(8,128)(2,1)}, bf16[768,768]{1,0:T(8,128)(2,1)}, bf16[768,768]{1,0:T(8,128)(2,1)}, f32[32,768]{1,0:T(8,128)}, /*index=5*/f32[2,8,768]{2,1,0:T(8,128)}) custom-call(f32[2048,768]{1,0:T(8,128)} %bitcast.36, f32[2,1,768]{2,1,0:T(1,128)} %reshape.232.row_ref, ...), custom_call_target="tpu_custom_call" | custom-call | tf_op jit(solution)/shard_map/last/pallas_call | solution.py:259
  432.6 0.7 reduce-scatter.7.cloned.1.call-update
  433.4 0.7 reduce-scatter.9.cloned.1.call-update
  434.1 0.5 reduce-scatter.13.cloned.1.call-update
  434.7 0.7 reduce-scatter.15.cloned.1.call-update
  435.5 0.5 reduce-scatter.17.cloned.1.call-update
  436.0 25.2 %reduce-scatter.11.cloned.1.call-done = bf16[192,768]{1,0:T(8,128)(2,1)} async-done(((bf16[768,768]{1,0:T(8,128)(2,1)}), bf16[192,768]{1,0:T(8,128)(2,1)}) %reduce-scatter.11.cloned.1.call-update) | async-done | bytes 294928 | tf_op jit(solution)/shard_map/reduce_scatter | solution.py:296
  461.3 32.1 %reduce-scatter.7.cloned.1.call-done = bf16[192,768]{1,0:T(8,128)(2,1)} async-done(((bf16[768,768]{1,0:T(8,128)(2,1)}), bf16[192,768]{1,0:T(8,128)(2,1)}) %reduce-scatter.7.cloned.1.call-update) | async-done | bytes 294928 | tf_op jit(solution)/shard_map/reduce_scatter | solution.py:296
  493.3 32.1 %reduce-scatter.9.cloned.1.call-done = bf16[192,768]{1,0:T(8,128)(2,1)} async-done(((bf16[768,768]{1,0:T(8,128)(2,1)}), bf16[192,768]{1,0:T(8,128)(2,1)}) %reduce-scatter.9.cloned.1.call-update) | async-done | bytes 294928 | tf_op jit(solution)/shard_map/reduce_scatter | solution.py:296
  525.4 31.9 %reduce-scatter.13.cloned.1.call-done = bf16[192,768]{1,0:T(8,128)(2,1)} async-done(((bf16[768,768]{1,0:T(8,128)(2,1)}), bf16[192,768]{1,0:T(8,128)(2,1)}) %reduce-scatter.13.cloned.1.call-update) | async-done | bytes 294928 | tf_op jit(solution)/shard_map/reduce_scatter | solution.py:296
  557.3 60.1 %reduce-scatter.15.cloned.1.call-done = bf16[192,3072]{1,0:T(8,128)(2,1)} async-done(((bf16[768,3072]{1,0:T(8,128)(2,1)}), bf16[192,3072]{1,0:T(8,128)(2,1)}) %reduce-scatter.15.cloned.1.call-update) | async-done | bytes 1179664 | tf_op jit(solution)/shard_map/reduce_scatter | solution.py:296
  617.4 60.0 %reduce-scatter.17.cloned.1.call-done = bf16[768,768]{1,0:T(8,128)(2,1)} async-done(((bf16[3072,768]{1,0:T(8,128)(2,1)}), bf16[768,768]{1,0:T(8,128)(2,1)}) %reduce-scatter.17.cloned.1.call-update) | async-done | bytes 1179664 | tf_op jit(solution)/shard_map/reduce_scatter | solution.py:296
  678.1 0.2 dynamic-update-slice.1
  678.4 40.9 %all-reduce.1 = s32[64]{0:T(128)S(1)} all-reduce(s32[64]{0:T(128)S(1)} %dynamic-update-slice.1), channel_id=1, replica_groups=mesh['rep'=8,'shard'=4] {'rep','shard'}, use_global_device_ids=true, to_apply=%add.1 | all-reduce | flops 64 | bytes 512
  719.4 0.1 convert_element_type.175
  719.5 16.7 %all-reduce.7 = (bf16[4,8,192]{2,1,0:T(8,128)(2,1)S(1)}, bf16[3072]{0:T(1024)(128)(2,1)S(1)}) all-reduce(bf16[4,8,192]{2,1,0:T(8,128)(2,1)S(1)} %copy.38, bf16[3072]{0:T(1024)(128)(2,1)S(1)} %reduce_sum.39), channel_id=4, replica_groups=mesh['rep'=8,'shard'=4] {'shard'}, use_global_device_ids=true, to_apply=%region_4.5.clone | all-reduce | flops 9216 | bytes 36864
  736.3 0.6 constant_dynamic-slice_fusion
  736.9 14.4 %all-reduce.5 = (bf16[1,8,192]{2,1,0:T(8,128)(2,1)S(1)}, bf16[768]{0:T(1024)(128)(2,1)S(1)}) all-reduce(bf16[1,8,192]{2,1,0:T(8,128)(2,1)S(1)} %constant_dynamic-slice_fusion, bf16[768]{0:T(1024)(128)(2,1)S(1)} %dynamic-slice.6), channel_id=1, replica_groups=mesh['rep'=8,'shard'=4] {'rep'}, use_global_device_ids=true, to_apply=%region_5.6 | all-reduce | flops 2304 | bytes 9216 | tf_op jit(solution)/shard_map/psum | solution.py:299
  751.4 0.6 convert_element_type.184
  752.0 64.3 %all-gather.2 = bf16[32,2,768]{2,1,0:T(2,128)(2,1)S(1)} all-gather(bf16[1,2,768]{2,1,0:T(2,128)(2,1)S(1)} %bitcast.44), channel_id=1, replica_groups=mesh['rep'=8,'shard'=4] {'rep','shard'}, dimensions={0}, use_global_device_ids=true | all-gather | bytes 101376 | tf_op jit(solution)/shard_map/all_gather | solution.py:301
  816.3 0.6 fusion.6
  816.9 1.5 fusion.2
  818.5 3.1 convert_element_type.182
  821.6 1.6 convert_element_type.185
  823.1 0.9 convert_element_type.178
  824.0 0.9 convert_element_type.179
  824.8 0.9 convert_element_type.180
  825.7 0.9 convert_element_type.181
  (86 shorter events, 1.1 us)
Async XLA Ops:
  7.2 4.1 copy-start.10
  7.2 5.4 copy-start.20
  7.2 14.4 %copy-start.12 = (bf16[192]{0:T(256)(128)(2,1)S(1)}, bf16[192]{0:T(256)(128)(2,1)}, u32[]{:S(2)}) copy-start(bf16[192]{0:T(256)(128)(2,1)} %param.24) | copy-start | bytes 1156
  7.2 14.4 %copy-start.13 = (bf16[192]{0:T(256)(128)(2,1)S(1)}, bf16[192]{0:T(256)(128)(2,1)}, u32[]{:S(2)}) copy-start(bf16[192]{0:T(256)(128)(2,1)} %param.25) | copy-start | bytes 1156
  7.2 14.4 %copy-start.14 = (bf16[192]{0:T(256)(128)(2,1)S(1)}, bf16[192]{0:T(256)(128)(2,1)}, u32[]{:S(2)}) copy-start(bf16[192]{0:T(256)(128)(2,1)} %param.27) | copy-start | bytes 1156
  7.2 14.4 %copy-start.15 = (bf16[192]{0:T(256)(128)(2,1)S(1)}, bf16[192]{0:T(256)(128)(2,1)}, u32[]{:S(2)}) copy-start(bf16[192]{0:T(256)(128)(2,1)} %param.30) | copy-start | bytes 1156
  7.3 14.4 %copy-start.16 = (bf16[192]{0:T(256)(128)(2,1)S(1)}, bf16[192]{0:T(256)(128)(2,1)}, u32[]{:S(2)}) copy-start(bf16[192]{0:T(256)(128)(2,1)} %param.32) | copy-start | bytes 1156
  7.3 14.4 %copy-start.17 = (bf16[192]{0:T(256)(128)(2,1)S(1)}, bf16[192]{0:T(256)(128)(2,1)}, u32[]{:S(2)}) copy-start(bf16[192]{0:T(256)(128)(2,1)} %param.33) | copy-start | bytes 1156
  7.3 14.4 %copy-start.18 = (bf16[192]{0:T(256)(128)(2,1)S(1)}, bf16[192]{0:T(256)(128)(2,1)}, u32[]{:S(2)}) copy-start(bf16[192]{0:T(256)(128)(2,1)} %param.34) | copy-start | bytes 1156
  7.3 14.4 %copy-start.11 = (bf16[768]{0:T(1024)(128)(2,1)S(1)}, bf16[768]{0:T(1024)(128)(2,1)}, u32[]{:S(2)}) copy-start(bf16[768]{0:T(1024)(128)(2,1)} %param.36) | copy-start | bytes 4612
  7.3 14.4 %copy-start.19 = (bf16[192]{0:T(256)(128)(2,1)S(1)}, bf16[192]{0:T(256)(128)(2,1)}, u32[]{:S(2)}) copy-start(bf16[192]{0:T(256)(128)(2,1)} %param.38) | copy-start | bytes 1156
  7.3 41.5 %copy-start.9 = (s32[2,1024]{1,0:T(2,128)S(1)}, s32[2,1024]{1,0:T(2,128)}, u32[]{:S(2)}) copy-start(s32[2,1024]{1,0:T(2,128)} %param.21) | copy-start | bytes 24580
  7.3 46.0 %all-gather.10.cloned.1.call-start = ((), (), s32[]{:S(2)}) async-start(), calls=%async_computation.6 | async-start | bytes 1474560 | tf_op jit(solution)/shard_map/all_gather | solution.py:271
  8.1 62.4 %all-gather.12.cloned.1.call-start = ((), (), s32[]{:S(2)}) async-start(), calls=%async_computation.7 | async-start | bytes 1474560 | tf_op jit(solution)/shard_map/all_gather | solution.py:271
  8.8 91.2 %all-gather.14.cloned.1.call-start = ((), (), s32[]{:S(2)}) async-start(), calls=%async_computation.8 | async-start | bytes 1474560 | tf_op jit(solution)/shard_map/all_gather | solution.py:271
  9.5 144.9 %all-gather.16.cloned.1.call-start = ((), (), s32[]{:S(2)}) async-start(), calls=%async_computation.9 | async-start | bytes 1474560 | tf_op jit(solution)/shard_map/all_gather | solution.py:271
  10.1 178.2 %all-gather.18.cloned.1.call-start = ((), (), s32[]{:S(2)}) async-start(), calls=%async_computation.10 | async-start | bytes 5898240 | tf_op jit(solution)/shard_map/all_gather | solution.py:271
  10.7 236.4 %all-gather.20.cloned.1.call-start = ((), (), s32[]{:S(2)}) async-start(), calls=%async_computation.11 | async-start | bytes 5898240 | tf_op jit(solution)/shard_map/all_gather | solution.py:271
  11.3 450.0 %reduce-scatter.11.cloned.1.call-start = ((), (), s32[]{:S(2)}) async-start(), calls=%async_computation.14 | async-start | bytes 1474560 | tf_op jit(solution)/shard_map/reduce_scatter | solution.py:296
  432.6 60.8 %reduce-scatter.7.cloned.1.call-start = ((), (), s32[]{:S(2)}) async-start(), calls=%async_computation.12 | async-start | bytes 1474560 | tf_op jit(solution)/shard_map/reduce_scatter | solution.py:296
  433.3 92.1 %reduce-scatter.9.cloned.1.call-start = ((), (), s32[]{:S(2)}) async-start(), calls=%async_computation.13 | async-start | bytes 1474560 | tf_op jit(solution)/shard_map/reduce_scatter | solution.py:296
  434.1 123.2 %reduce-scatter.13.cloned.1.call-start = ((), (), s32[]{:S(2)}) async-start(), calls=%async_computation.15 | async-start | bytes 1474560 | tf_op jit(solution)/shard_map/reduce_scatter | solution.py:296
  434.7 182.8 %reduce-scatter.15.cloned.1.call-start = ((), (), s32[]{:S(2)}) async-start(), calls=%async_computation.16 | async-start | bytes 5898240 | tf_op jit(solution)/shard_map/reduce_scatter | solution.py:296
  435.4 242.0 %reduce-scatter.17.cloned.1.call-start = ((), (), s32[]{:S(2)}) async-start(), calls=%async_computation.17 | async-start | bytes 5898240 | tf_op jit(solution)/shard_map/reduce_scatter | solution.py:296
  435.4 242.7 %copy-start.21 = (s32[2]{0:T(128)S(1)}, s32[2]{0:T(128)}, u32[]{:S(2)}) copy-start(s32[2]{0:T(128)} %param.22) | copy-start | bytes 28
  435.5 283.8 %copy-start.7 = (f32[32,768]{1,0:T(8,128)S(1)}, f32[32,768]{1,0:T(8,128)}, u32[]{:S(2)}) copy-start(f32[32,768]{1,0:T(8,128)} %get-tuple-element.53) | copy-start | bytes 294916
  435.5 283.8 %copy-start.6 = (f32[32,768]{1,0:T(8,128)S(1)}, f32[32,768]{1,0:T(8,128)}, u32[]{:S(2)}) copy-start(f32[32,768]{1,0:T(8,128)} %get-tuple-element.54) | copy-start | bytes 294916
  435.5 284.0 %copy-start.5 = (f32[8,3072]{1,0:T(8,128)S(1)}, f32[8,3072]{1,0:T(8,128)}, u32[]{:S(2)}) copy-start(f32[8,3072]{1,0:T(8,128)} %get-tuple-element.60) | copy-start | bytes 294916
  436.0 316.0 %copy-start.8 = (f32[2,8,768]{2,1,0:T(8,128)S(1)}, f32[2,8,768]{2,1,0:T(8,128)}, u32[]{:S(2)}) copy-start(f32[2,8,768]{2,1,0:T(8,128)} %get-tuple-element.52) | copy-start | bytes 147460
  436.0 382.5 %all-reduce.10.cloned.1.call-start = ((), (), s32[]{:S(2)}) async-start(), calls=%async_computation.18 | async-start | bytes 7077888 | tf_op jit(solution)/shard_map/psum | solution.py:296
  818.5 3.1 copy-start
  818.5 4.7 copy-start.4
  818.5 5.5 copy-start.3
  821.5 3.3 copy-start.2
  821.5 4.2 copy-start.1
Sparse Core Ops, SparseCore 0:
  10.0 30.7 all-gather.9
  42.6 27.7 all-gather.11
  72.3 27.7 all-gather.13
  101.7 27.7 all-gather.15
  131.2 57.0 all-gather.17
  190.0 57.0 all-gather.19
  432.7 28.5 reduce-scatter.10
  464.8 28.5 reduce-scatter.6
  496.8 28.5 reduce-scatter.8
  528.7 28.5 reduce-scatter.12
  560.3 57.0 reduce-scatter.14
  620.3 57.0 reduce-scatter.16
  680.3 87.7 all-reduce.9

commit v2 on v1

v2 whole, which is shorter than its diff:
```python
import functools
import math

import jax
import jax.numpy as jnp
from jax import lax
from jax.experimental import pallas as pl
from jax.experimental.pallas import tpu as pltpu
from jax.sharding import PartitionSpec as P

NEG=-1e30
EPS=1e-5
L=1024
D=768
FF=3072
HC=D//2
BF=jnp.bfloat16
F32=jnp.float32
LOG2E=math.log2(math.e)
LN2=math.log(2.0)
QS=0.125*LOG2E
ANY=pl.BlockSpec(memory_space=pl.ANY)
S_=jax.ShapeDtypeStruct


def nt(a,b):
    return lax.dot_general(a,b,(((1,),(1,)),((),())),preferred_element_type=F32)


def nn(a,b):
    return lax.dot_general(a,b,(((1,),(0,)),((),())),preferred_element_type=F32)


def tn(a,b):
    return lax.dot_general(a,b,(((0,),(0,)),((),())),preferred_element_type=F32)


def full(*s):
    return pl.BlockSpec(s,lambda i,*_:(0,)*len(s),pipeline_mode=pl.Buffered(1))


def norm(x):
    mean=jnp.mean(x,axis=1,keepdims=True)
    off=x-mean
    var=jnp.mean(off*off,axis=1,keepdims=True)
    r=lax.rsqrt(var+EPS)
    return off*r,r


def sum8(x):
    return jnp.sum(x.reshape(x.shape[0]//8,8,x.shape[1]),axis=0)


def cost(flops,nbytes,trans=0):
    return pl.CostEstimate(flops=int(flops),bytes_accessed=int(nbytes),transcendentals=int(trans))


def seg_features(seg):
    lane=jnp.arange(128)%64
    hit=seg[:,None]==lane[None,:]
    first=(lane<4)[None]
    fq=jnp.where(first&hit,1.0,0.0).astype(BF)
    fk=jnp.where(first,jnp.where(hit,0.0,NEG),jnp.where((lane<7)[None],1.0,0.0)).astype(BF)
    return fq,fk


def qkv_kernel(idx_ref,*refs,ns,wr):
    tok_ref,row_ref,vec_ref=refs[:3]
    own=refs[3:6]
    mine=refs[6:5+ns]
    other=refs[5+ns:4+2*ns]
    hi=4+2*ns
    mine=refs[6:6+ns-1]
    other=refs[6+ns-1:6+2*(ns-1)]
    hi=6+2*(ns-1)
    q_ref,k_ref,v_ref,w_ref,sem=refs[hi:hi+5]
    @pl.when(pl.program_id(0)==0)
    def _():
        c=idx_ref[0]
        cps=[]
        def put(src,w,sh,c0,nc):
            dst=w_ref.at[w,pl.ds(pl.multiple_of(sh*wr,16),wr),pl.ds(c0,nc)]
            cp=pltpu.make_async_copy(src,dst,sem.at[len(cps)])
            cp.start()
            cps.append(cp)
        for w in range(3):
            put(own[w],w,idx_ref[1],0,D)
        for j in range(1,ns):
            for w in range(3):
                put(mine[j-1].at[pl.ds(w*wr,wr)],w,idx_ref[1+j],pl.multiple_of(c*HC,128),HC)
                put(other[j-1].at[pl.ds(w*wr,wr)],w,idx_ref[1+ns+j],pl.multiple_of((1-c)*HC,128),HC)
        for cp in cps:
            cp.wait()
    xhat,_=norm(tok_ref[...]+row_ref[0])
    n1=(xhat*vec_ref[0:1,:]+vec_ref[1:2,:]).astype(BF)
    q_ref[...]=((nn(n1,w_ref[0])+vec_ref[2:3,:])*QS).astype(BF)
    k_ref[...]=nn(n1,w_ref[1]).astype(BF)
    v_ref[...]=(nn(n1,w_ref[2])+vec_ref[3:4,:]).astype(BF)


def qkv(idx,tok,row,vec,own,mine,other,tb=512):
    T=tok.shape[0]
    per=L//tb
    ns=len(mine)+1
    wr=own[0].shape[0]
    blk=pl.BlockSpec((tb,D),lambda i,*_:(i,0))
    return pl.pallas_call(
        functools.partial(qkv_kernel,ns=ns,wr=wr),
        grid_spec=pltpu.PrefetchScalarGridSpec(
            num_scalar_prefetch=1,grid=(T//tb,),
            in_specs=[blk,pl.BlockSpec((1,1,D),lambda i,*_:(i//per,0,0)),full(8,D)]+[ANY]*(3+2*(ns-1)),
            out_specs=[blk]*3+[full(3,D,D)],
            scratch_shapes=[pltpu.SemaphoreType.DMA((3+6*(ns-1),))]),
        out_shape=[S_((T,D),BF)]*3+[S_((3,D,D),BF)],
        compiler_params=pltpu.CompilerParams(dimension_semantics=("arbitrary",)),
        cost_estimate=cost(6*T*D*D,T*D*10+9*D*D),
        name="qkv")(idx,tok,row,vec,*own,*mine,*other)


def fwd_kernel(q_ref,k_ref,v_ref,fq_ref,fk_ref,*refs,qb):
    o_ref,fx_ref=refs[-2:]
    lane=lax.broadcasted_iota(jnp.int32,(1,128),1)
    lo=lane<64
    l6=lane&63
    ks=[]
    vs=[]
    k=k_ref[...]
    v=v_ref[...]
    fk=fk_ref[...]
    for h in (0,1):
        own=lo if h==0 else ~lo
        ks.append(jnp.where(own,k,fk))
        vs.append(jnp.where(own,v,jnp.where(l6==0,1.0,0.0).astype(BF)))
    for b in range(L//qb):
        rows=pl.ds(b*qb,qb)
        q=q_ref[rows,:]
        fq=fq_ref[rows,:]
        accs=[]
        ls=[]
        for h in (0,1):
            own=lo if h==0 else ~lo
            s=nt(jnp.where(own,q,fq),ks[h])
            m=jnp.max(s,axis=1,keepdims=True)
            p=jnp.exp2(s-m).astype(BF)
            acc=nn(p,vs[h])
            l=acc[:,64:65] if h==0 else acc[:,0:1]
            accs.append(acc*(1.0/l))
            ls.append(-(m+jnp.log2(l)))
        o_ref[rows,:]=jnp.where(lo,accs[0],accs[1]).astype(BF)
        nl=jnp.where(lo,ls[1],ls[0])
        hi=nl.astype(BF).astype(F32)
        r1=nl-hi
        mid=r1.astype(BF).astype(F32)
        r2=r1-mid
        fx_ref[rows,:]=jnp.where(l6==4,hi,jnp.where(l6==5,mid,jnp.where(l6==6,r2,fq.astype(F32)))).astype(BF)


def attn_fwd(q,k,v,fq,fk,prev,s0,ns,p0,npair,qb=512):
    T=q.shape[0]
    blk=pl.BlockSpec((L,128),lambda s,p:(s0+s,p0+p))
    fb=pl.BlockSpec((L,128),lambda s,p:(s0+s,0))
    n=ns*npair
    prev=list(prev)
    return pl.pallas_call(
        functools.partial(fwd_kernel,qb=qb),grid=(ns,npair),
        in_specs=[blk,blk,blk,fb,fb]+[ANY]*len(prev),out_specs=[blk,blk],
        out_shape=[S_((T,D),BF)]*2,
        input_output_aliases={5+i:i for i in range(len(prev))},
        compiler_params=pltpu.CompilerParams(dimension_semantics=("arbitrary","arbitrary")),
        cost_estimate=cost(n*2*4*L*L*256,n*L*128*14,n*2*L*L),
        name="attn_fwd")(q,k,v,fq,fk,*prev)


def bwd_kernel(q_ref,k_ref,v_ref,fx_ref,fk_ref,o_ref,do_ref,*refs,qb):
    dq_ref,dk_ref,dv_ref=refs[-3:]
    lane=lax.broadcasted_iota(jnp.int32,(1,128),1)
    lo=lane<64
    l6=lane&63
    zero=jnp.zeros((),BF)
    ones2=jnp.where(l6<2,1.0,0.0).astype(BF)
    k=k_ref[...]
    v=v_ref[...]
    fk=fk_ref[...]
    kx=[]
    vx=[]
    km=[]
    for h in (0,1):
        own=lo if h==0 else ~lo
        kx.append(jnp.where(own,k,fk))
        vx.append(jnp.where(own,v,ones2))
        km.append(jnp.where(own,k,zero))
    dv=jnp.zeros((L,128),F32)
    dk=jnp.zeros((L,128),F32)
    for b in range(L//qb):
        rows=pl.ds(b*qb,qb)
        q=q_ref[rows,:]
        fx=fx_ref[rows,:]
        do=do_ref[rows,:]
        prod=do.astype(F32)*o_ref[rows,:].astype(F32)
        d0=-jnp.sum(jnp.where(lo,prod,0.0),axis=1,keepdims=True)
        d1=-jnp.sum(jnp.where(lo,0.0,prod),axis=1,keepdims=True)
        nd=jnp.where(lo,d1,d0)
        hi=nd.astype(BF).astype(F32)
        fd=jnp.where(l6==0,hi,jnp.where(l6==1,nd-hi,0.0)).astype(BF)
        dq=jnp.zeros((qb,128),F32)
        for h in (0,1):
            own=lo if h==0 else ~lo
            qx=jnp.where(own,q,fx)
            dx=jnp.where(own,do,fd)
            qm=jnp.where(own,q,zero)
            dm=jnp.where(own,do,zero)
            p=jnp.exp2(nt(kx[h],qx))
            dpt=nt(vx[h],dx)
            pb=p.astype(BF)
            ds=(p*dpt).astype(BF)
            dv=dv+nn(pb,dm)
            dk=dk+nn(ds,qm)
            dq=dq+tn(ds,km[h])
        dq_ref[rows,:]=(dq*0.125).astype(BF)
    dv_ref[...]=dv.astype(BF)
    dk_ref[...]=(dk*LN2).astype(BF)


def attn_bwd(q,k,v,fx,fk,o,do,prev,s0,ns,p0,npair,qb=256):
    T=q.shape[0]
    blk=pl.BlockSpec((L,128),lambda s,p:(s0+s,p0+p))
    fb=pl.BlockSpec((L,128),lambda s,p:(s0+s,0))
    n=ns*npair
    prev=list(prev)
    return pl.pallas_call(
        functools.partial(bwd_kernel,qb=qb),grid=(ns,npair),
        in_specs=[blk,blk,blk,blk,fb,blk,blk]+[ANY]*len(prev),out_specs=[blk]*3,
        out_shape=[S_((T,D),BF)]*3,
        input_output_aliases={7+i:i for i in range(len(prev))},
        compiler_params=pltpu.CompilerParams(dimension_semantics=("arbitrary","arbitrary")),
        cost_estimate=cost(n*2*10*L*L*256,n*L*128*20,n*2*L*L),
        name="attn_bwd")(q,k,v,fx,fk,o,do,*prev)


def mid_kernel(idx_ref,*refs,tb,fc,ns,wr,fr):
    tok_ref,row_ref,att_ref,cot_ref,vec_ref,ub_ref=refs[:6]
    own=refs[6:9]
    mine=refs[9:9+ns-1]
    other=refs[9+ns-1:9+2*(ns-1)]
    b0=9+2*(ns-1)
    res_ref,gm_ref,ga_ref,keep_ref,send_ref,sv_ref,sub_ref,ow,up,dn,aup,adn,aow,sem=refs[b0:]
    i=pl.program_id(0)
    n=pl.num_programs(0)
    c=idx_ref[0]
    def copies():
        cps=[]
        def put(src,dst):
            cps.append(pltpu.make_async_copy(src,dst,sem.at[len(cps)]))
        r16=lambda sh,m: pl.ds(pl.multiple_of(sh*m,16),m)
        sh=idx_ref[1]
        put(own[0],ow.at[r16(sh,wr)])
        put(own[1],up.at[r16(sh,wr)])
        put(own[2],dn.at[r16(sh,fr)])
        for j in range(1,ns):
            for src,sh,cc in ((mine[j-1],idx_ref[1+j],c),(other[j-1],idx_ref[1+ns+j],1-c)):
                cd=pl.ds(pl.multiple_of(cc*HC,128),HC)
                put(src.at[pl.ds(0,wr)],ow.at[r16(sh,wr),cd])
                for b in range(4):
                    put(src.at[pl.ds(wr+b*wr,wr)],up.at[r16(sh,wr),pl.ds(pl.multiple_of(cc*4*HC+b*HC,128),HC)])
                put(src.at[pl.ds(5*wr,fr)],dn.at[r16(sh,fr),cd])
        return cps
    @pl.when(i==0)
    def _():
        cps=copies()
        for cp in cps:
            cp.start()
        aup[...]=jnp.zeros_like(aup)
        adn[...]=jnp.zeros_like(adn)
        aow[...]=jnp.zeros_like(aow)
        sv_ref[...]=jnp.zeros_like(sv_ref)
        sub_ref[...]=jnp.zeros_like(sub_ref)
        for cp in cps:
            cp.wait()
    ob=vec_ref[0:1,:]
    g2=vec_ref[1:2,:]
    b2=vec_ref[2:3,:]
    db=vec_ref[3:4,:]
    att=att_ref[...]
    mixed=tok_ref[...]+row_ref[0]+nn(att,ow[...])+ob
    xhat,r=norm(mixed)
    n2=(xhat*g2+b2).astype(BF)
    n2t=n2.T
    cot=cot_ref[...]
    g=cot.astype(BF)
    res=mixed+db
    gn2=jnp.zeros((tb,D),F32)
    for j in range(FF//fc):
        cs=slice(j*fc,(j+1)*fc)
        pre=nn(n2,up[:,cs])+ub_ref[:,cs]
        gact=nt(g,dn[cs,:])
        phi=0.5+0.5*lax.erf(pre*(2**-0.5))
        pdf=jnp.exp2(pre*pre*(-0.5*LOG2E))*(1.0/math.sqrt(2*math.pi))
        act=(pre*phi).astype(BF)
        gp=gact*(phi+pre*pdf)
        gpre=gp.astype(BF)
        sub_ref[:,cs]+=sum8(gp)
        res=res+nn(act,dn[cs,:])
        gn2=gn2+nt(gpre,up[:,cs])
        adn[cs,:]+=tn(act,g)
        aup[:,cs]+=nn(n2t,gpre)
    res_ref[...]=res
    e=gn2*g2
    c1=jnp.mean(e,axis=1,keepdims=True)
    c2=jnp.mean(e*xhat,axis=1,keepdims=True)
    gm=cot+r*(e-c1-xhat*c2)
    gml=gm.astype(BF)
    gm_ref[...]=gml
    ga_ref[...]=nt(gml,ow[...]).astype(BF)
    aow[...]+=tn(att,gml)
    sv_ref[0:8,:]+=sum8(gm)
    sv_ref[8:16,:]+=sum8(gn2*xhat)
    sv_ref[16:24,:]+=sum8(gn2)
    sv_ref[24:32,:]+=sum8(cot)
    @pl.when(i==n-1)
    def _():
        for ref,base,odd in ((keep_ref,1,0),(send_ref,1+ns,1)):
            for ch in (0,1):
                @pl.when(c==(ch+odd)%2)
                def _():
                    def body(j,carry):
                        sh=idx_ref[base+j]
                        rw=pl.ds(pl.multiple_of(sh*wr,8),wr)
                        ref[j,0:wr,:]=aow[rw,ch*HC:(ch+1)*HC].astype(BF)
                        for b in range(4):
                            lo=(ch*4+b)*HC
                            ref[j,wr+b*wr:2*wr+b*wr,:]=aup[rw,lo:lo+HC].astype(BF)
                        ref[j,5*wr:5*wr+fr,:]=adn[pl.ds(pl.multiple_of(sh*fr,8),fr),ch*HC:(ch+1)*HC].astype(BF)
                        return carry
                    lax.fori_loop(0,ns,body,0)


def mid(idx,tok,row,att,cot,vec,ub,own,mine,other,tb=256,fc=512):
    T=tok.shape[0]
    per=L//tb
    ns=len(mine)+1
    wr=own[0].shape[0]
    fr=own[2].shape[0]
    rb=5*wr+fr
    blk=pl.BlockSpec((tb,D),lambda i,*_:(i,0))
    return pl.pallas_call(
        functools.partial(mid_kernel,tb=tb,fc=fc,ns=ns,wr=wr,fr=fr),
        grid_spec=pltpu.PrefetchScalarGridSpec(
            num_scalar_prefetch=1,grid=(T//tb,),
            in_specs=[blk,pl.BlockSpec((1,1,D),lambda i,*_:(i//per,0,0)),blk,blk,full(8,D),full(1,FF)]+[ANY]*(3+2*(ns-1)),
            out_specs=[blk,blk,blk,full(ns,rb,HC),full(ns,rb,HC),full(32,D),full(8,FF)],
            scratch_shapes=[pltpu.VMEM((D,D),BF),pltpu.VMEM((D,FF),BF),pltpu.VMEM((FF,D),BF),
                pltpu.VMEM((D,FF),F32),pltpu.VMEM((FF,D),F32),pltpu.VMEM((D,D),F32),
                pltpu.SemaphoreType.DMA((3+12*(ns-1),))]),
        out_shape=[S_((T,D),F32),S_((T,D),BF),S_((T,D),BF),S_((ns,rb,HC),BF),S_((ns,rb,HC),BF),S_((32,D),F32),S_((8,FF),F32)],
        compiler_params=pltpu.CompilerParams(dimension_semantics=("arbitrary",),vmem_limit_bytes=67043328),
        cost_estimate=cost(6*T*D*(D+2*FF),T*D*20+30*D*FF,2*T*FF),
        name="mid")(idx,tok,row,att,cot,vec,ub,*own,*mine,*other)


def dw_kernel(idx_ref,tok_ref,row_ref,dq_ref,dk_ref,dv_ref,vec_ref,keep_ref,send_ref,sv_ref,acc,*,ns,wr):
    i=pl.program_id(0)
    c=idx_ref[0]
    @pl.when(i==0)
    def _():
        acc[...]=jnp.zeros_like(acc)
        sv_ref[...]=jnp.zeros_like(sv_ref)
    xhat,_=norm(tok_ref[...]+row_ref[0])
    n1t=(xhat*vec_ref[0:1,:]+vec_ref[1:2,:]).astype(BF).T
    for w,ref in enumerate((dq_ref,dk_ref,dv_ref)):
        acc[w]+=nn(n1t,ref[...])
    sv_ref[0:8,:]+=sum8(dq_ref[...].astype(F32))
    sv_ref[8:16,:]+=sum8(dv_ref[...].astype(F32))
    @pl.when(i==pl.num_programs(0)-1)
    def _():
        for ref,base,odd in ((keep_ref,1,0),(send_ref,1+ns,1)):
            for ch in (0,1):
                @pl.when(c==(ch+odd)%2)
                def _():
                    def body(j,carry):
                        rw=pl.ds(pl.multiple_of(idx_ref[base+j]*wr,8),wr)
                        for w in range(3):
                            ref[j,w*wr:(w+1)*wr,:]=acc[w,rw,ch*HC:(ch+1)*HC].astype(BF)
                        return carry
                    lax.fori_loop(0,ns,body,0)


def dw(idx,tok,row,dq,dk,dv,vec,ns,tb=512):
    T=tok.shape[0]
    per=L//tb
    wr=D//ns
    blk=pl.BlockSpec((tb,D),lambda i,*_:(i,0))
    return pl.pallas_call(
        functools.partial(dw_kernel,ns=ns,wr=wr),
        grid_spec=pltpu.PrefetchScalarGridSpec(
            num_scalar_prefetch=1,grid=(T//tb,),
            in_specs=[blk,pl.BlockSpec((1,1,D),lambda i,*_:(i//per,0,0)),blk,blk,blk,full(8,D)],
            out_specs=[full(ns,3*wr,HC),full(ns,3*wr,HC),full(16,D)],
            scratch_shapes=[pltpu.VMEM((3,D,D),F32)]),
        out_shape=[S_((ns,3*wr,HC),BF)]*2+[S_((16,D),F32)],
        compiler_params=pltpu.CompilerParams(dimension_semantics=("arbitrary",)),
        cost_estimate=cost(6*T*D*D,T*D*10+12*D*D),
        name="dw")(idx,tok,row,dq,dk,dv,vec)


def dx_kernel(tok_ref,row_ref,dq_ref,dk_ref,dv_ref,gm_ref,w_ref,vec_ref,gt_ref,sv_ref,ts_ref,*,per):
    i=pl.program_id(0)
    @pl.when(i==0)
    def _():
        sv_ref[...]=jnp.zeros_like(sv_ref)
    @pl.when(i%per==0)
    def _():
        ts_ref[...]=jnp.zeros_like(ts_ref)
    gn=nt(dq_ref[...],w_ref[0])+nt(dk_ref[...],w_ref[1])+nt(dv_ref[...],w_ref[2])
    xhat,r=norm(tok_ref[...]+row_ref[0])
    e=gn*vec_ref[0:1,:]
    c1=jnp.mean(e,axis=1,keepdims=True)
    c2=jnp.mean(e*xhat,axis=1,keepdims=True)
    gt=gm_ref[...].astype(F32)+r*(e-c1-xhat*c2)
    gt_ref[...]=gt
    sv_ref[0:8,:]+=sum8(gn*xhat)
    sv_ref[8:16,:]+=sum8(gn)
    ts_ref[0]+=sum8(gt)


def dx(tok,row,dq,dk,dv,gm,w,vec,tb=512):
    T=tok.shape[0]
    per=L//tb
    blk=pl.BlockSpec((tb,D),lambda i:(i,0))
    return pl.pallas_call(
        functools.partial(dx_kernel,per=per),grid=(T//tb,),
        in_specs=[blk,pl.BlockSpec((1,1,D),lambda i:(i//per,0,0)),blk,blk,blk,blk,full(3,D,D),full(8,D)],
        out_specs=[blk,full(16,D),pl.BlockSpec((1,8,D),lambda i:(i//per,0,0))],
        out_shape=[S_((T,D),F32),S_((16,D),F32),S_((T//L,8,D),F32)],
        compiler_params=pltpu.CompilerParams(dimension_semantics=("arbitrary",)),
        cost_estimate=cost(6*T*D*D,T*D*16+6*D*D),
        name="dx")(tok,row,dq,dk,dv,gm,w,vec)


class Ring:
    def __init__(self,rep,shard):
        self.R,self.S=rep,shard
        self.nb=shard.bit_length()-1
        self.Z=rep//2
        r=lax.axis_index("rep")
        self.s=lax.axis_index("shard")
        self.c=r%2
        self.z=r//2

    def move(self,x,to):
        pairs=[]
        for r in range(self.R):
            for s in range(self.S):
                r2,s2=to(r,s)
                pairs.append((r*self.S+s,r2*self.S+s2))
        return lax.ppermute(x,("rep","shard"),pairs)

    def order(self,c,t):
        return (t+c*(self.nb//2))%self.nb

    def mask(self,c,j):
        m=0
        for t in range(self.nb):
            if j>>t&1:
                m|=1<<self.order(c,t)
        return m

    def step(self,x,t):
        return self.move(x,lambda r,s:(r,s^(1<<self.order(r%2,t))))

    def direct(self,x,j):
        return self.move(x,lambda r,s:(r,s^j))

    def core(self,x):
        return self.move(x,lambda r,s:(r^1,s))

    def plane(self,x,j):
        return self.move(x,lambda r,s:(r^(2*j),s))

    def index(self,order_free):
        m=[],[]
        for c in (0,1):
            for j in range(self.S):
                m[c].append(j if order_free else self.mask(c,j))
        t=jnp.array([m[0],m[1]],jnp.int32)
        mine=t[self.c]^self.s
        other=t[1-self.c]^self.s
        return jnp.concatenate([self.c[None],mine,other]).astype(jnp.int32)


def add(a,b):
    return (a.astype(F32)+b.astype(F32)).astype(BF)


def reduce_all(g,keep,send):
    got=g.core(send)
    n=g.S
    x=keep
    for t in reversed(range(g.nb)):
        n//=2
        if got is None:
            up,x=x[n:],x[:n]
        else:
            up,x=add(x[n:],got[n:]),add(x[:n],got[:n])
        got=g.step(up,t)
    x=add(x[0],got[0]).reshape(g.Z,-1,HC)
    mine=lax.dynamic_index_in_dim(x,g.z,0,keepdims=False).astype(F32)
    parts=[g.plane(lax.dynamic_index_in_dim(x,g.z^j,0,keepdims=False),j) for j in range(1,g.Z)]
    for p in parts:
        mine=mine+p.astype(F32)
    mine=mine.astype(BF)
    back=[mine]+[g.plane(mine,j) for j in range(1,g.Z)]
    out=jnp.zeros(x.shape,BF)
    for j in range(g.Z):
        out=lax.dynamic_update_index_in_dim(out,back[j],g.z^j,0)
    out=out.reshape(-1,HC)
    other=g.core(out)
    first=jnp.where(g.c==0,out,other).astype(F32)
    second=jnp.where(g.c==0,other,out).astype(F32)
    return first,second


def local(tokens,segments,time_steps,time_table,ln1_gain,ln1_bias,q_weight,q_bias,k_weight,v_weight,v_bias,o_weight,o_bias,ln2_gain,ln2_bias,up_weight,up_bias,down_weight,down_bias,cotangent):
    nseq=tokens.shape[0]
    T=nseq*L
    g=Ring(lax.axis_size("rep"),lax.axis_size("shard"))
    S=g.S
    w=ln1_gain.shape[0]
    fr=down_weight.shape[0]
    own=time_table.shape[0]
    half=lambda x,b=0: lax.dynamic_slice_in_dim(x,(g.c*(x.shape[1]//D)*HC) + b*HC,HC,1)
    st=jnp.concatenate([time_steps//32,time_steps%32]).astype(BF)
    small=jnp.concatenate([ln1_gain,ln1_bias,q_bias,v_bias,o_bias,ln2_gain,ln2_bias,down_bias,up_bias,st])
    smalls=jnp.stack([small]+[g.direct(small,j) for j in range(1,S)])
    pack_a=jnp.concatenate([half(q_weight),half(k_weight),half(v_weight)])
    mine_a=[g.direct(pack_a,j) for j in range(1,S)]
    steps=smalls[:,-2*nseq:].astype(jnp.int32)
    steps=steps[:,:nseq]*32+steps[:,nseq:]
    idx=steps-g.s*own
    inside=(idx>=0)&(idx<own)
    rows=jnp.where(inside[:,:,None],time_table[jnp.clip(idx,0,own-1)],jnp.zeros((),BF))
    row=rows[0].astype(F32)
    for j in range(1,S):
        row=row+g.direct(rows[j],j).astype(F32)
    row=row.reshape(nseq,1,D)
    sm=jnp.take(smalls[:,:smalls.shape[1]-2*nseq],jnp.arange(S)^g.s,axis=0).astype(F32)
    vecs=[sm[:,i*w:(i+1)*w].reshape(-1) for i in range(8)]
    ub=sm[:,8*w:].reshape(1,-1)
    g1,b1,qb,vb,ob,g2,b2,db=vecs
    z=jnp.zeros_like(g1)
    vec1=jnp.stack([g1,b1,qb,vb,z,z,z,z])
    vec2=jnp.stack([ob,g2,b2,db,z,z,z,z])
    other_a=[g.core(x) for x in mine_a]
    pack_b=jnp.concatenate([half(o_weight)]+[half(up_weight,b) for b in range(4)]+[half(down_weight)])
    pack_b,*mine_a=lax.optimization_barrier((pack_b,*mine_a))
    tok=tokens.reshape(T,D)
    cot=cotangent.reshape(T,D)
    fq,fk=seg_features(segments.reshape(T))
    idx_a=g.index(True)
    idx_b=g.index(False)
    q,k,v,wqkv=qkv(idx_a,tok,row,vec1,(q_weight,k_weight,v_weight),mine_a,other_a)
    mine_b=[pack_b]
    for t in range(g.nb):
        mine_b=mine_b+[g.step(x,t) for x in mine_b]
    other_b=[g.core(x) for x in mine_b[1:]]
    fwd=()
    for s in range(nseq):
        for p in (0,3):
            fwd=attn_fwd(q,k,v,fq,fk,fwd,s,1,p,3)
    att,fx=fwd
    res,gm,ga,keep_b,send_b,sv2,sub=mid(idx_b,tok,row,att,cot,vec2,ub,(o_weight,up_weight,down_weight),mine_b[1:],other_b)
    first_b,second_b=reduce_all(g,keep_b,send_b)
    bwd=()
    for s in range(nseq):
        for p in (0,3):
            bwd=attn_bwd(q,k,v,fx,fk,att,ga,bwd,s,1,p,3)
    dq,dk,dv=bwd
    keep_a,send_a,svq=dw(idx_b,tok,row,dq,dk,dv,vec1,S)
    first_a,second_a=reduce_all(g,keep_a,send_a)
    gt,sv1,ts=dx(tok,row,dq,dk,dv,gm,wqkv,vec1)
    s8=lambda x: x.reshape(-1,8,D).sum(1)
    vs=jnp.concatenate([s8(sv1),s8(svq),s8(sv2)]).reshape(-1,S,w).transpose(1,0,2).reshape(S,-1)
    vs=jnp.concatenate([vs,sub.sum(0).reshape(S,-1)],1).astype(BF)
    tsum=ts.sum(1).astype(BF)
    st=jnp.concatenate([tsum.reshape(-1),st])
    pieces=[lax.dynamic_index_in_dim(vs,g.s,0,keepdims=False)]
    tss=[st]
    for j in range(1,S):
        got=g.direct(jnp.concatenate([lax.dynamic_index_in_dim(vs,g.s^j,0,keepdims=False),st]),j)
        pieces.append(got[:vs.shape[1]])
        tss.append(got[vs.shape[1]:])
    mine_v=sum(x.astype(F32) for x in pieces).astype(BF)
    pay=jnp.concatenate([mine_v]+tss)
    alls=[pay]+[g.move(pay,lambda r,s,j=j:(r^j,s)) for j in range(1,g.R)]
    alls=order_rep(g,alls)
    tot=sum(x[:vs.shape[1]].astype(F32) for x in alls)
    sums=tot[:8*w].reshape(8,w)
    subs=tot[8*w:]
    tt=jnp.stack([x[vs.shape[1]:].reshape(S,-1) for x in alls])
    rows_t=tt[:,:,:nseq*D].reshape(-1,D)
    sids=tt[:,:,nseq*D:].astype(jnp.int32)
    sids=(sids[:,:,:nseq]*32+sids[:,:,nseq:]).reshape(-1)
    ids=g.s*own+jnp.arange(own)
    gtab=jnp.dot((ids[:,None]==sids[None,:]).astype(BF),rows_t,preferred_element_type=F32)
    def unpack(r0,nr):
        return jnp.concatenate([first_a[r0:r0+nr],second_a[r0:r0+nr]],1)
    gq,gk,gv=(unpack(i*w,w) for i in range(3))
    go=jnp.concatenate([first_b[:w],second_b[:w]],1)
    gup=jnp.concatenate([x[w+b*w:w+(b+1)*w] for x in (first_b,second_b) for b in range(4)],1)
    gdn=jnp.concatenate([first_b[5*w:],second_b[5*w:]],1)
    return (res.reshape(tokens.shape),gt.reshape(tokens.shape),gtab,sums[0],sums[1],gq,sums[2],gk,gv,sums[3],go,sums[4],sums[5],sums[6],gup,subs,gdn,sums[7])


def order_rep(g,alls):
    st=jnp.take(jnp.stack(alls),jnp.arange(g.R)^(2*g.z+g.c),axis=0)
    return [st[i] for i in range(g.R)]


def solution(mesh):
    b=("rep","shard")
    s=P("shard")
    m=P("shard",None)
    t=P(b,None,None)
    return jax.shard_map(local,mesh=mesh,
        in_specs=(t,P(b,None),P(b),m,s,s,m,s,m,m,s,m,s,s,s,m,s,m,s,t),
        out_specs=(t,t,m,s,s,m,s,m,m,s,m,s,s,s,m,s,m,s),check_vma=False)
```

time: 834 us -> 531 us (0.64)
  waiting for transfers between devices: 387 us -> 123 us
  blocking collectives: 168 us -> 0 us
  starting transfers between devices: 0.5 us -> 55.8 us
  local copies, waits for them, and re-layouts: 7.72 us -> 39.2 us
  Pallas kernels: 240 us -> 268 us
  other arithmetic: 11.3 us -> 33.5 us
  between operations: 16.2 us -> 1.8 us
    reduce_scatter x6 -> x0, waiting for transfers between devices: 241 us -> none  [red(): lax.psum_scatter(x, 'shard', scatter_dimension=0, tiled=True)]
    all_gather x6 -> x0, waiting for transfers between devices: 139 us -> none  [local(): ag = lambda x: lax.all_gather(x, 'shard', axis=0, tiled=True)]
    ppermute x0 -> x48, waiting for transfers between devices: none -> 123 us  [move(): return lax.ppermute(x, ('rep', 'shard'), pairs)]
    unnamed x4 -> x0, blocking collectives: 81.6 us -> none
    all_gather x2 -> x0, blocking collectives: 72.4 us -> none  [the longest x1 64.3 us: local(): lax.all_gather(ts.sum(1).astype(BF), ('rep', 'shard'), axis=0, tiled=True)]
    ppermute x0 -> x48, starting transfers between devices: none -> 55.8 us  [move(): return lax.ppermute(x, ('rep', 'shard'), pairs)]
    pallas_call x5 -> x12, Pallas kernels: 240 us -> 268 us  [the longest x1 90.6 us: mid(): pl.pallas_call(functools.partial(mid_kernel, tb=tb, fc=fc, ns=ns, wr=wr,...]
    psum x1 -> x0, blocking collectives: 14.4 us -> none  [local(): lax.psum(lax.psum_scatter(allv, 'shard', scatter_dimension=0, tiled=True)...]
  transfers between devices with their start and end apart: 13 -> 48, of which waited for: 10 -> 15; matrix products, arithmetic and copies ran while one was open for 1% -> 13% of each run, Pallas kernels for 7% -> 34%
where the time goes in v2:
time: 531 us; the launch traced here: 523 us
  Pallas kernels  268 us (50%)
  waiting for transfers between devices  123 us (23%)
  starting transfers between devices  55.8 us (11%)
  local copies, waits for them, and re-layouts  39.2 us (7%)
  other arithmetic  33.5 us (6%)
    ppermute x48, waiting for transfers between devices, move(): return lax.ppermute(x, ('rep', 'shard'), pairs)  123 us
    pallas_call x1, Pallas kernels, mid(): pl.pallas_call(functools.partial(mid_kernel, tb=tb, fc=fc, ns=ns, wr=wr,...  90.6 us
    pallas_call x4, Pallas kernels, attn_bwd(): pl.pallas_call(functools.partial(bwd_kernel, qb=qb), grid=(ns, npair), in...  79.7 us
    ppermute x48, starting transfers between devices, move(): return lax.ppermute(x, ('rep', 'shard'), pairs)  55.8 us
    pallas_call x4, Pallas kernels, attn_fwd(): pl.pallas_call(functools.partial(fwd_kernel, qb=qb), grid=(ns, npair), in...  48.7 us
    pallas_call x1, Pallas kernels, dw(): pl.pallas_call(functools.partial(dw_kernel, ns=ns, wr=wr), grid_spec=pltp...  17.2 us
    convert_element_type x6, other arithmetic, add(): return (a.astype(F32) + b.astype(F32)).astype(BF)  16.6 us
    pallas_call x1, Pallas kernels, dx(): pl.pallas_call(functools.partial(dx_kernel, per=per), grid=(T // tb,), in...  15.9 us
  transfers between devices with their start and end apart: 48, of which 15 were waited for; matrix products, arithmetic and copies ran while one was open for 13% of the time, Pallas kernels for 34%

profile of v2, /device:TPU:0, one launch (start us, length us, event | category | flops | bytes accessed | tf_op | source)
XLA Modules:
  0.0 522.8 jit_solution(3083331129901196899)
XLA Ops:
  0.7 1.1 constant_dynamic-slice_fusion.2
  2.9 3.0 collective-permute-start.6
  5.9 1.5 collective-permute-start.7
  8.1 6.1 %concatenate.66 = bf16[2308]{0:T(1024)(128)(2,1)S(1)} concatenate(bf16[192]{0:T(256)(128)(2,1)} %param.26, bf16[192]{0:T(256)(128)(2,1)} %param.27, bf16[192]{0:T(256)(128)(2,1)} %param.29, bf16[192]{0:T(256)(128)(2,1)} %param.32, bf16[192]{0:T(256)(128)(2,1)} %param.34, bf16[192]{0:T(256)(128)(2,1)} %param.35, bf16[192]{0:T(256)(128)(2,1)} %param.36, bf16[192]{0:T(256)(128)(2,1)} %param.40, ...), dimensions={0} | concatenate | bytes 9232 | tf_op jit(solution)/shard_map/concatenate | solution.py:532
  14.8 2.9 collective-permute-start.2
  17.8 1.6 dynamic-slice_dynamic-update-slice_fusion.5
  20.1 1.1 select_convert_fusion.2.fq_ref
  21.2 1.1 fusion.1.fk_ref
  28.1 1.8 gather_fusion
  30.0 2.0 collective-permute-start.3
  32.1 1.5 collective-permute-start.4
  33.6 5.6 %collective-permute-done.8.refs_8_ = bf16[576,384]{1,0:T(8,128)(2,1)S(1)} collective-permute-done((bf16[576,384]{1,0:T(8,128)(2,1)S(1)}, bf16[576,384]{1,0:T(8,128)(2,1)S(1)}, u32[]{:S(2)}, u32[]{:S(2)}) %collective-permute-start.8) | collective-permute-done | bytes 442400 | tf_op jit(solution)/shard_map/ppermute | solution.py:455
  44.1 23.4 %collective-permute-done.12.refs_9_ = bf16[1728,384]{1,0:T(8,128)(2,1)S(1)} collective-permute-done((bf16[1728,384]{1,0:T(8,128)(2,1)}, bf16[1728,384]{1,0:T(8,128)(2,1)S(1)}, u32[]{:S(2)}, u32[]{:S(2)}) %collective-permute-start.12) | collective-permute-done | bytes 1327136 | tf_op jit(solution)/shard_map/ppermute | solution.py:455
  69.7 15.5 %qkv.1 = (bf16[2048,768]{1,0:T(8,128)(2,1)}, bf16[2048,768]{1,0:T(8,128)(2,1)}, bf16[2048,768]{1,0:T(8,128)(2,1)}, bf16[3,768,768]{2,1,0:T(8,128)(2,1)}) custom-call(s32[9]{0:T(128)} %pad_add_fusion.1.idx_ref, f32[2048,768]{1,0:T(8,128)} %bitcast.116, f32[2,1,768]{2,1,0:T(1,128)} %reshape.240.refs_1_.row_ref, f32[8,768]{1,0:T(8,128)} %stack.56.refs_2_.vec_ref, ...), custom_call_target="tpu_custom_call" | custom-call | flops 7247757312 | bytes 21037056 | tf_op jit(solution)/shard_map/qkv/pallas_call | solution.py:107
  85.2 12.0 %attn_fwd.4 = (bf16[2048,768]{1,0:T(8,128)(2,1)}, bf16[2048,768]{1,0:T(8,128)(2,1)}) custom-call(bf16[2048,768]{1,0:T(8,128)(2,1)} %get-tuple-element.62.q_ref, bf16[2048,768]{1,0:T(8,128)(2,1)} %get-tuple-element.63.k_ref, bf16[2048,768]{1,0:T(8,128)(2,1)} %get-tuple-element.64.v_ref, bf16[2048,128]{1,0:T(8,128)(2,1)} %select_convert_fusion.2.fq_ref, ...), custom_call_target="tpu_custom_call" | custom-call | flops 6442450944 | bytes 5505024 | tf_op jit(solution)/shard_map/attn_fwd/pallas_call | solution.py:164
  97.8 12.1 %attn_fwd.5 = (bf16[2048,768]{1,0:T(8,128)(2,1)}, bf16[2048,768]{1,0:T(8,128)(2,1)}) custom-call(bf16[2048,768]{1,0:T(8,128)(2,1)} %get-tuple-element.62.q_ref, bf16[2048,768]{1,0:T(8,128)(2,1)} %get-tuple-element.63.k_ref, bf16[2048,768]{1,0:T(8,128)(2,1)} %get-tuple-element.64.v_ref, ...), custom_call_target="tpu_custom_call", output_to_operand_aliasing={{0}: (5, {}), {1}: (6, {})} | custom-call | flops 6442450944 | bytes 5505024 | tf_op jit(solution)/shard_map/attn_fwd/pallas_call | solution.py:164
  109.9 12.6 %attn_fwd.6 = (bf16[2048,768]{1,0:T(8,128)(2,1)}, bf16[2048,768]{1,0:T(8,128)(2,1)}) custom-call(bf16[2048,768]{1,0:T(8,128)(2,1)} %get-tuple-element.62.q_ref, bf16[2048,768]{1,0:T(8,128)(2,1)} %get-tuple-element.63.k_ref, bf16[2048,768]{1,0:T(8,128)(2,1)} %get-tuple-element.64.v_ref, ...), custom_call_target="tpu_custom_call", output_to_operand_aliasing={{0}: (5, {}), {1}: (6, {})} | custom-call | flops 6442450944 | bytes 5505024 | tf_op jit(solution)/shard_map/attn_fwd/pallas_call | solution.py:164
  122.5 12.0 %attn_fwd.7 = (bf16[2048,768]{1,0:T(8,128)(2,1)}, bf16[2048,768]{1,0:T(8,128)(2,1)}) custom-call(bf16[2048,768]{1,0:T(8,128)(2,1)} %get-tuple-element.62.q_ref, bf16[2048,768]{1,0:T(8,128)(2,1)} %get-tuple-element.63.k_ref, bf16[2048,768]{1,0:T(8,128)(2,1)} %get-tuple-element.64.v_ref, ...), custom_call_target="tpu_custom_call", output_to_operand_aliasing={{0}: (5, {}), {1}: (6, {})} | custom-call | flops 6442450944 | bytes 5505024 | tf_op jit(solution)/shard_map/attn_fwd/pallas_call | solution.py:164
  135.6 90.6 %mid.1 = (f32[2048,768]{1,0:T(8,128)}, bf16[2048,768]{1,0:T(8,128)(2,1)}, bf16[2048,768]{1,0:T(8,128)(2,1)}, bf16[4,1728,384]{2,1,0:T(8,128)(2,1)}, bf16[4,1728,...) custom-call(s32[9]{0:T(128)} %pad_add_fusion.idx_ref, f32[2048,768]{1,0:T(8,128)} %bitcast.117, ...), custom_call_target="tpu_custom_call" | custom-call | flops 65229815808 | bytes 102236160 | tf_op jit(solution)/shard_map/mid/pallas_call | solution.py:345
  226.7 20.0 %attn_bwd.4 = (bf16[2048,768]{1,0:T(8,128)(2,1)}, bf16[2048,768]{1,0:T(8,128)(2,1)}, bf16[2048,768]{1,0:T(8,128)(2,1)}) custom-call(bf16[2048,768]{1,0:T(8,128)(2,1)} %get-tuple-element.62.q_ref, bf16[2048,768]{1,0:T(8,128)(2,1)} %get-tuple-element.63.k_ref, bf16[2048,768]{1,0:T(8,128)(2,1)} %get-tuple-element.64.v_ref, ...), custom_call_target="tpu_custom_call" | custom-call | flops 16106127360 | bytes 7864320 | tf_op jit(solution)/shard_map/attn_bwd/pallas_call | solution.py:230
  246.7 19.7 %attn_bwd.5 = (bf16[2048,768]{1,0:T(8,128)(2,1)}, bf16[2048,768]{1,0:T(8,128)(2,1)}, bf16[2048,768]{1,0:T(8,128)(2,1)}) custom-call(bf16[2048,768]{1,0:T(8,128)(2,1)} %get-tuple-element.62.q_ref, bf16[2048,768]{1,0:T(8,128)(2,1)} %get-tuple-element.63.k_ref, ...), custom_call_target="tpu_custom_call", output_to_operand_aliasing={{0}: (7, {}), {1}: (8, {}), {2}: (9, {})} | custom-call | flops 16106127360 | bytes 7864320 | tf_op jit(solution)/shard_map/attn_bwd/pallas_call | solution.py:230
  266.5 20.2 %attn_bwd.6 = (bf16[2048,768]{1,0:T(8,128)(2,1)}, bf16[2048,768]{1,0:T(8,128)(2,1)}, bf16[2048,768]{1,0:T(8,128)(2,1)}) custom-call(bf16[2048,768]{1,0:T(8,128)(2,1)} %get-tuple-element.62.q_ref, bf16[2048,768]{1,0:T(8,128)(2,1)} %get-tuple-element.63.k_ref, ...), custom_call_target="tpu_custom_call", output_to_operand_aliasing={{0}: (7, {}), {1}: (8, {}), {2}: (9, {})} | custom-call | flops 16106127360 | bytes 7864320 | tf_op jit(solution)/shard_map/attn_bwd/pallas_call | solution.py:230
  286.6 19.8 %attn_bwd.7 = (bf16[2048,768]{1,0:T(8,128)(2,1)}, bf16[2048,768]{1,0:T(8,128)(2,1)}, bf16[2048,768]{1,0:T(8,128)(2,1)}) custom-call(bf16[2048,768]{1,0:T(8,128)(2,1)} %get-tuple-element.62.q_ref, bf16[2048,768]{1,0:T(8,128)(2,1)} %get-tuple-element.63.k_ref, ...), custom_call_target="tpu_custom_call", output_to_operand_aliasing={{0}: (7, {}), {1}: (8, {}), {2}: (9, {})} | custom-call | flops 16106127360 | bytes 7864320 | tf_op jit(solution)/shard_map/attn_bwd/pallas_call | solution.py:230
  306.4 17.2 %dw.1 = (bf16[4,576,384]{2,1,0:T(8,128)(2,1)}, bf16[4,576,384]{2,1,0:T(8,128)(2,1)}, f32[16,768]{1,0:T(8,128)}) custom-call(s32[9]{0:T(128)} %pad_add_fusion.idx_ref, f32[2048,768]{1,0:T(8,128)} %bitcast.118, f32[2,1,768]{2,1,0:T(1,128)} %reshape.240.refs_1_.row_ref, bf16[2048,768]{1,0:T(8,128)(2,1)} %get-tuple-element.85.dq_ref, ...), custom_call_target="tpu_custom_call" | custom-call | flops 7247757312 | bytes 22806528 | tf_op jit(solution)/shard_map/dw/pallas_call | solution.py:392
  324.5 15.9 %dx.1 = (f32[2048,768]{1,0:T(8,128)}, f32[16,768]{1,0:T(8,128)}, f32[2,8,768]{2,1,0:T(8,128)}) custom-call(f32[2048,768]{1,0:T(8,128)} %bitcast.119, f32[2,1,768]{2,1,0:T(1,128)} %reshape.240.refs_1_.row_ref, bf16[2048,768]{1,0:T(8,128)(2,1)} %get-tuple-element.85.dq_ref, bf16[2048,768]{1,0:T(8,128)(2,1)} %get-tuple-element.86.dk_ref, ...), custom_call_target="tpu_custom_call" | custom-call | flops 7247757312 | bytes 28704768 | tf_op jit(solution)/shard_map/dx/pallas_call | solution.py:429
  342.8 1.3 collective-permute-start.19
  344.2 2.1 collective-permute-start.20
  346.4 2.3 collective-permute-done.20
  348.9 1.6 collective-permute-start.22
  351.4 2.6 collective-permute-start.24
  354.0 3.6 collective-permute-start.26
  358.3 1.4 collective-permute-done.26
  359.7 2.9 collective-permute-done.27
  362.6 1.4 stack.66
  364.7 6.0 %add_convert_fusion.1 = (bf16[2,1728,384]{2,1,0:T(8,128)(2,1)S(1)}, bf16[2,1728,384]{2,1,0:T(8,128)(2,1)}) fusion(bf16[4,1728,384]{2,1,0:T(8,128)(2,1)} %collective-permute-done.38, bf16[4,1728,384]{2,1,0:T(8,128)(2,1)} %get-tuple-element.98), kind=kLoop, calls=%fused_computation.4 | loop fusion | flops 10616832 | bytes 15925248 | tf_op jit(solution)/shard_map/convert_element_type | solution.py:491
  371.4 1.1 slice_reduce_fusion
  377.4 3.3 add_convert_fusion.6
  380.7 1.5 collective-permute-start.29
  382.8 1.4 stack_reshape.62
  384.9 1.3 constant_dynamic-update-slice_fusion.3
  386.2 16.9 %collective-permute-done.39 = bf16[2,1728,384]{2,1,0:T(8,128)(2,1)} collective-permute-done((bf16[2,1728,384]{2,1,0:T(8,128)(2,1)}, bf16[2,1728,384]{2,1,0:T(8,128)(2,1)}, u32[]{:S(2)}, u32[]{:S(2)}) %collective-permute-start.39) | collective-permute-done | bytes 2654240 | tf_op jit(solution)/shard_map/ppermute | solution.py:455
  403.2 2.7 add_convert_fusion.3
  405.9 2.0 collective-permute-start.40
  407.9 8.9 %collective-permute-done.29 = bf16[2,576,384]{2,1,0:T(8,128)(2,1)} collective-permute-done((bf16[2,576,384]{2,1,0:T(8,128)(2,1)}, bf16[2,576,384]{2,1,0:T(8,128)(2,1)}, u32[]{:S(2)}, u32[]{:S(2)}) %collective-permute-start.29) | collective-permute-done | bytes 884768 | tf_op jit(solution)/shard_map/ppermute | solution.py:455
  416.8 1.1 add_convert_fusion.8
  417.9 2.4 collective-permute-start.30
  421.6 9.4 %collective-permute-done.30 = bf16[1,576,384]{2,1,0:T(8,128)(2,1)S(1)} collective-permute-done((bf16[1,576,384]{2,1,0:T(8,128)(2,1)S(1)}, bf16[1,576,384]{2,1,0:T(8,128)(2,1)S(1)}, u32[]{:S(2)}, u32[]{:S(2)}) %collective-permute-start.30) | collective-permute-done | bytes 442400 | tf_op jit(solution)/shard_map/ppermute | solution.py:455
  431.0 1.2 add_convert_fusion.7
  433.0 1.1 collective-permute-start.32
  434.1 3.3 collective-permute-start.33
  439.5 5.2 collective-permute-done.32
  445.7 2.4 collective-permute-start.34
  448.1 2.2 add_convert_fusion.2
  450.6 1.9 collective-permute-start.42
  452.5 2.4 collective-permute-start.43
  454.9 1.5 fusion.5
  456.5 1.5 collective-permute-start.36
  458.1 7.2 %collective-permute-done.41 = bf16[432,384]{1,0:T(8,128)(2,1)S(1)} collective-permute-done((bf16[432,384]{1,0:T(8,128)(2,1)S(1)}, bf16[432,384]{1,0:T(8,128)(2,1)S(1)}, u32[]{:S(2)}, u32[]{:S(2)}) %collective-permute-start.41) | collective-permute-done | bytes 331808 | tf_op jit(solution)/shard_map/ppermute | solution.py:455
  465.2 16.0 %collective-permute-done.42 = bf16[432,384]{1,0:T(8,128)(2,1)S(1)} collective-permute-done((bf16[432,384]{1,0:T(8,128)(2,1)S(1)}, bf16[432,384]{1,0:T(8,128)(2,1)S(1)}, u32[]{:S(2)}, u32[]{:S(2)}) %collective-permute-start.42) | collective-permute-done | bytes 331808 | tf_op jit(solution)/shard_map/ppermute | solution.py:455
  481.6 7.7 %collective-permute-start.44 = (bf16[432,384]{1,0:T(8,128)(2,1)S(1)}, bf16[432,384]{1,0:T(8,128)(2,1)S(1)}, u32[]{:S(2)}, u32[]{:S(2)}) collective-permute-start(bf16[432,384]{1,0:T(8,128)(2,1)S(1)} %get-tuple-element.112), channel_id=1, source_target_pairs={{0,8},{1,9},{2,10},{3,11},{4,12},{5,13},{6,14},{7,15},{8,0},{9,1},... | collective-permute-start | bytes 995336 | tf_op jit(solution)/shard_map/ppermute | solution.py:455
  490.5 1.5 collective-permute-start.46
  492.0 8.2 %collective-permute-done.44 = bf16[432,384]{1,0:T(8,128)(2,1)S(1)} collective-permute-done((bf16[432,384]{1,0:T(8,128)(2,1)S(1)}, bf16[432,384]{1,0:T(8,128)(2,1)S(1)}, u32[]{:S(2)}, u32[]{:S(2)}) %collective-permute-start.44) | collective-permute-done | bytes 331808 | tf_op jit(solution)/shard_map/ppermute | solution.py:455
  500.3 13.9 %collective-permute-done.45 = bf16[432,384]{1,0:T(8,128)(2,1)S(1)} collective-permute-done((bf16[432,384]{1,0:T(8,128)(2,1)S(1)}, bf16[432,384]{1,0:T(8,128)(2,1)S(1)}, u32[]{:S(2)}, u32[]{:S(2)}) %collective-permute-start.45) | collective-permute-done | bytes 331808 | tf_op jit(solution)/shard_map/ppermute | solution.py:455
  519.6 1.8 pad_maximum_fusion
  (246 shorter events, 44.1 us)
Async XLA Ops:
  0.7 22.2 %copy-start.1 = (bf16[192,3072]{1,0:T(8,128)(2,1)S(1)}, bf16[192,3072]{1,0:T(8,128)(2,1)}, u32[]{:S(2)}) copy-start(bf16[192,3072]{1,0:T(8,128)(2,1)} %refs_7_.1) | copy-start | bytes 3538948
  0.7 24.9 %copy-start.2 = (bf16[768,768]{1,0:T(8,128)(2,1)S(1)}, bf16[768,768]{1,0:T(8,128)(2,1)}, u32[]{:S(2)}) copy-start(bf16[768,768]{1,0:T(8,128)(2,1)} %refs_8_.1) | copy-start | bytes 3538948
  2.8 23.6 %copy-start.14 = (s32[2,4]{1,0:T(2,128)S(1)}, s32[2,4]{1,0:T(2,128)}, u32[]{:S(2)}) copy-start(s32[2,4]{1,0:T(2,128)} %constant.198.clone) | copy-start | bytes 100
  2.8 23.6 %copy-start.15 = (s32[2,4]{1,0:T(2,128)S(1)}, s32[2,4]{1,0:T(2,128)}, u32[]{:S(2)}) copy-start(s32[2,4]{1,0:T(2,128)} %constant.199.clone) | copy-start | bytes 100
  2.9 30.7 %collective-permute-start.6 = (bf16[576,384]{1,0:T(8,128)(2,1)S(1)}, bf16[576,384]{1,0:T(8,128)(2,1)S(1)}, u32[]{:S(2)}, u32[]{:S(2)}) collective-permute-start(bf16[576,384]{1,0:T(8,128)(2,1)S(1)} %pad_maximum_fusion.5), channel_id=1, source_target_pairs={{0,1},{1,0},{2,3},{3,2},{4,5},{5,4},{6,7},{7,6},{8,9},{9,8},{10,11... | collective-permute-start | bytes 1327112 | tf_op jit(solution)/shard_map/ppermute | solution.py:455
  5.9 27.7 %collective-permute-start.7 = (bf16[576,384]{1,0:T(8,128)(2,1)S(1)}, bf16[576,384]{1,0:T(8,128)(2,1)}, u32[]{:S(2)}, u32[]{:S(2)}) collective-permute-start(bf16[576,384]{1,0:T(8,128)(2,1)S(1)} %pad_maximum_fusion.5), channel_id=1, source_target_pairs={{0,2},{1,3},{2,0},{3,1},{4,6},{5,7},{6,4},{7,5},{8,10},{9,11},{10,... | collective-permute-start | bytes 1327112 | tf_op jit(solution)/shard_map/ppermute | solution.py:455
  8.1 35.0 %copy-start.9 = (bf16[2]{0:T(256)(128)(2,1)}, bf16[2]{0:T(256)(128)(2,1)S(1)}, u32[]{:S(2)}) copy-start(bf16[2]{0:T(256)(128)(2,1)S(1)} %get-tuple-element.162) | copy-start | bytes 16
  8.1 35.0 %copy-start.11 = (bf16[2]{0:T(256)(128)(2,1)}, bf16[2]{0:T(256)(128)(2,1)S(1)}, u32[]{:S(2)}) copy-start(bf16[2]{0:T(256)(128)(2,1)S(1)} %get-tuple-element.163) | copy-start | bytes 16
  14.2 13.5 %collective-permute-start = (bf16[2308]{0:T(1024)(128)(2,1)S(1)}, bf16[2308]{0:T(1024)(128)(2,1)S(1)}, u32[]{:S(2)}, u32[]{:S(2)}) collective-permute-start(bf16[2308]{0:T(1024)(128)(2,1)S(1)} %concatenate.66), channel_id=1, source_target_pairs={{0,1},{1,0},{2,3},{3,2},{4,5},{5,4},{6,7},{7,6},{8,9},{9,8},{10,11... | collective-permute-start | bytes 13856 | tf_op jit(solution)/shard_map/ppermute | solution.py:455
  14.8 13.0 %collective-permute-start.1 = (bf16[2308]{0:T(1024)(128)(2,1)S(1)}, bf16[2308]{0:T(1024)(128)(2,1)S(1)}, u32[]{:S(2)}, u32[]{:S(2)}) collective-permute-start(bf16[2308]{0:T(1024)(128)(2,1)S(1)} %concatenate.66), channel_id=1, source_target_pairs={{0,2},{1,3},{2,0},{3,1},{4,6},{5,7},{6,4},{7,5},{8,10},{9,11},{10,... | collective-permute-start | bytes 13856 | tf_op jit(solution)/shard_map/ppermute | solution.py:455
  14.8 13.0 %collective-permute-start.2 = (bf16[2308]{0:T(1024)(128)(2,1)S(1)}, bf16[2308]{0:T(1024)(128)(2,1)S(1)}, u32[]{:S(2)}, u32[]{:S(2)}) collective-permute-start(bf16[2308]{0:T(1024)(128)(2,1)S(1)} %concatenate.66), channel_id=1, source_target_pairs={{0,3},{1,2},{2,1},{3,0},{4,7},{5,6},{6,5},{7,4},{8,11},{9,10},{10,... | collective-permute-start | bytes 13856 | tf_op jit(solution)/shard_map/ppermute | solution.py:455
  27.7 11.6 %collective-permute-start.8 = (bf16[576,384]{1,0:T(8,128)(2,1)S(1)}, bf16[576,384]{1,0:T(8,128)(2,1)S(1)}, u32[]{:S(2)}, u32[]{:S(2)}) collective-permute-start(bf16[576,384]{1,0:T(8,128)(2,1)S(1)} %pad_maximum_fusion.5), channel_id=1, source_target_pairs={{0,3},{1,2},{2,1},{3,0},{4,7},{5,6},{6,5},{7,4},{8,11},{9,10},{10,... | collective-permute-start | bytes 1327112 | tf_op jit(solution)/shard_map/ppermute | solution.py:455
  30.0 10.6 %collective-permute-start.3 = (bf16[2,768]{1,0:T(2,128)(2,1)S(1)}, bf16[2,768]{1,0:T(2,128)(2,1)S(1)}, u32[]{:S(2)}, u32[]{:S(2)}) collective-permute-start(bf16[2,768]{1,0:T(2,128)(2,1)S(1)} %get-tuple-element.147), channel_id=1, source_target_pairs={{0,1},{1,0},{2,3},{3,2},{4,5},{5,4},{6,7},{7,6},{8,9},{9,8},{10,11... | collective-permute-start | bytes 9224 | tf_op jit(solution)/shard_map/ppermute | solution.py:455
  32.1 9.1 %collective-permute-start.4 = (bf16[2,768]{1,0:T(2,128)(2,1)S(1)}, bf16[2,768]{1,0:T(2,128)(2,1)S(1)}, u32[]{:S(2)}, u32[]{:S(2)}) collective-permute-start(bf16[2,768]{1,0:T(2,128)(2,1)S(1)} %get-tuple-element.149), channel_id=1, source_target_pairs={{0,2},{1,3},{2,0},{3,1},{4,6},{5,7},{6,4},{7,5},{8,10},{9,11},{10,... | collective-permute-start | bytes 9224 | tf_op jit(solution)/shard_map/ppermute | solution.py:455
  33.6 35.2 %copy-start.19 = (bf16[576,384]{1,0:T(8,128)(2,1)}, bf16[576,384]{1,0:T(8,128)(2,1)S(1)}, u32[]{:S(2)}) copy-start(bf16[576,384]{1,0:T(8,128)(2,1)S(1)} %collective-permute-done.6.refs_6_) | copy-start | bytes 1327108
  33.6 10.2 %collective-permute-start.5 = (bf16[2,768]{1,0:T(2,128)(2,1)S(1)}, bf16[2,768]{1,0:T(2,128)(2,1)S(1)}, u32[]{:S(2)}, u32[]{:S(2)}) collective-permute-start(bf16[2,768]{1,0:T(2,128)(2,1)S(1)} %get-tuple-element.148), channel_id=1, source_target_pairs={{0,3},{1,2},{2,1},{3,0},{4,7},{5,6},{6,5},{7,4},{8,11},{9,10},{10,... | collective-permute-start | bytes 9224 | tf_op jit(solution)/shard_map/ppermute | solution.py:455
  39.3 29.5 %copy-start.20 = (bf16[576,384]{1,0:T(8,128)(2,1)}, bf16[576,384]{1,0:T(8,128)(2,1)S(1)}, u32[]{:S(2)}) copy-start(bf16[576,384]{1,0:T(8,128)(2,1)S(1)} %collective-permute-done.8.refs_8_) | copy-start | bytes 1327108
  39.3 28.2 %collective-permute-start.12 = (bf16[1728,384]{1,0:T(8,128)(2,1)}, bf16[1728,384]{1,0:T(8,128)(2,1)S(1)}, u32[]{:S(2)}, u32[]{:S(2)}) collective-permute-start(bf16[1728,384]{1,0:T(8,128)(2,1)} %dynamic-slice_dynamic-update-slice_fusion), channel_id=1, source_target_pairs={{0,1},{1,0},{2,3},{3,2},{4,6},{5,7},{6,4},{7,5},{8,9},{9,8},{10,11... | collective-permute-start | bytes 3981320 | tf_op jit(solution)/shard_map/ppermute | solution.py:455
  40.6 28.2 %collective-permute-start.10 = (bf16[576,384]{1,0:T(8,128)(2,1)}, bf16[576,384]{1,0:T(8,128)(2,1)S(1)}, u32[]{:S(2)}, u32[]{:S(2)}) collective-permute-start(bf16[576,384]{1,0:T(8,128)(2,1)} %collective-permute-done.7.refs_7_), channel_id=1, source_target_pairs={{0,4},{1,5},{2,6},{3,7},{4,0},{5,1},{6,2},{7,3},{8,12},{9,13},{10,... | collective-permute-start | bytes 1327112 | tf_op jit(solution)/shard_map/ppermute | solution.py:455
  40.6 28.1 %collective-permute-start.11 = (bf16[576,384]{1,0:T(8,128)(2,1)S(1)}, bf16[576,384]{1,0:T(8,128)(2,1)S(1)}, u32[]{:S(2)}, u32[]{:S(2)}) collective-permute-start(bf16[576,384]{1,0:T(8,128)(2,1)S(1)} %collective-permute-done.8.refs_8_), channel_id=1, source_target_pairs={{0,4},{1,5},{2,6},{3,7},{4,0},{5,1},{6,2},{7,3},{8,12},{9,13},{10,... | collective-permute-start | bytes 1327112 | tf_op jit(solution)/shard_map/ppermute | solution.py:455
  41.1 27.7 %collective-permute-start.9 = (bf16[576,384]{1,0:T(8,128)(2,1)S(1)}, bf16[576,384]{1,0:T(8,128)(2,1)}, u32[]{:S(2)}, u32[]{:S(2)}) collective-permute-start(bf16[576,384]{1,0:T(8,128)(2,1)S(1)} %collective-permute-done.6.refs_6_), channel_id=1, source_target_pairs={{0,4},{1,5},{2,6},{3,7},{4,0},{5,1},{6,2},{7,3},{8,12},{9,13},{10,... | collective-permute-start | bytes 1327112 | tf_op jit(solution)/shard_map/ppermute | solution.py:455
  43.8 53.5 %collective-permute-start.13 = (bf16[1728,384]{1,0:T(8,128)(2,1)}, bf16[1728,384]{1,0:T(8,128)(2,1)}, u32[]{:S(2)}, u32[]{:S(2)}) collective-permute-start(bf16[1728,384]{1,0:T(8,128)(2,1)} %dynamic-slice_dynamic-update-slice_fusion), channel_id=1, source_target_pairs={{0,2},{1,3},{2,0},{3,1},{4,5},{5,4},{6,7},{7,6},{8,10},{9,11},{10,... | collective-permute-start | bytes 3981320 | tf_op jit(solution)/shard_map/ppermute | solution.py:455
  67.5 29.7 %copy-start.17 = (bf16[1728,384]{1,0:T(8,128)(2,1)}, bf16[1728,384]{1,0:T(8,128)(2,1)S(1)}, u32[]{:S(2)}) copy-start(bf16[1728,384]{1,0:T(8,128)(2,1)S(1)} %collective-permute-done.12.refs_9_) | copy-start | bytes 3981316
  67.5 30.3 %collective-permute-start.14 = (bf16[1728,384]{1,0:T(8,128)(2,1)S(1)}, bf16[1728,384]{1,0:T(8,128)(2,1)}, u32[]{:S(2)}, u32[]{:S(2)}) collective-permute-start(bf16[1728,384]{1,0:T(8,128)(2,1)S(1)} %collective-permute-done.12.refs_9_), channel_id=1, source_target_pairs={{0,2},{1,3},{2,0},{3,1},{4,5},{5,4},{6,7},{7,6},{8,10},{9,11},{10,... | collective-permute-start | bytes 3981320 | tf_op jit(solution)/shard_map/ppermute | solution.py:455
  97.2 37.3 %collective-permute-start.15 = (bf16[1728,384]{1,0:T(8,128)(2,1)S(1)}, bf16[1728,384]{1,0:T(8,128)(2,1)S(1)}, u32[]{:S(2)}, u32[]{:S(2)}) collective-permute-start(bf16[1728,384]{1,0:T(8,128)(2,1)S(1)} %collective-permute-done.12.refs_9_), channel_id=1, source_target_pairs={{0,4},{1,5},{2,6},{3,7},{4,0},{5,1},{6,2},{7,3},{8,12},{9,13},{10,... | collective-permute-start | bytes 3981320 | tf_op jit(solution)/shard_map/ppermute | solution.py:455
  97.3 38.3 %collective-permute-start.16 = (bf16[1728,384]{1,0:T(8,128)(2,1)}, bf16[1728,384]{1,0:T(8,128)(2,1)}, u32[]{:S(2)}, u32[]{:S(2)}) collective-permute-start(bf16[1728,384]{1,0:T(8,128)(2,1)} %collective-permute-done.13.refs_10_), channel_id=1, source_target_pairs={{0,4},{1,5},{2,6},{3,7},{4,0},{5,1},{6,2},{7,3},{8,12},{9,13},{10,... | collective-permute-start | bytes 3981320 | tf_op jit(solution)/shard_map/ppermute | solution.py:455
  97.7 37.8 %collective-permute-start.17 = (bf16[1728,384]{1,0:T(8,128)(2,1)}, bf16[1728,384]{1,0:T(8,128)(2,1)}, u32[]{:S(2)}, u32[]{:S(2)}) collective-permute-start(bf16[1728,384]{1,0:T(8,128)(2,1)} %collective-permute-done.14.refs_11_), channel_id=1, source_target_pairs={{0,4},{1,5},{2,6},{3,7},{4,0},{5,1},{6,2},{7,3},{8,12},{9,13},{10,... | collective-permute-start | bytes 3981320 | tf_op jit(solution)/shard_map/ppermute | solution.py:455
  226.2 138.5 %collective-permute-start.38 = (bf16[4,1728,384]{2,1,0:T(8,128)(2,1)}, bf16[4,1728,384]{2,1,0:T(8,128)(2,1)}, u32[]{:S(2)}, u32[]{:S(2)}) collective-permute-start(bf16[4,1728,384]{2,1,0:T(8,128)(2,1)} %get-tuple-element.99), channel_id=1, source_target_pairs={{0,4},{1,5},{2,6},{3,7},{4,0},{5,1},{6,2},{7,3},{8,12},{9,13},{10,... | collective-permute-start | bytes 15925256 | tf_op jit(solution)/shard_map/ppermute | solution.py:455
  324.4 16.8 %copy-start.4 = (f32[32,768]{1,0:T(8,128)S(1)}, f32[32,768]{1,0:T(8,128)}, u32[]{:S(2)}) copy-start(f32[32,768]{1,0:T(8,128)} %get-tuple-element.93) | copy-start | bytes 294916
  324.5 17.1 %copy-start.3 = (f32[8,3072]{1,0:T(8,128)S(1)}, f32[8,3072]{1,0:T(8,128)}, u32[]{:S(2)}) copy-start(f32[8,3072]{1,0:T(8,128)} %get-tuple-element.94) | copy-start | bytes 294916
  324.5 18.1 %copy-start.10 = (bf16[2]{0:T(256)(128)(2,1)S(1)}, bf16[2]{0:T(256)(128)(2,1)}, u32[]{:S(2)}) copy-start(bf16[2]{0:T(256)(128)(2,1)} %copy-done.9) | copy-start | bytes 16
  324.5 18.1 %copy-start.12 = (bf16[2]{0:T(256)(128)(2,1)S(1)}, bf16[2]{0:T(256)(128)(2,1)}, u32[]{:S(2)}) copy-start(bf16[2]{0:T(256)(128)(2,1)} %copy-done.11) | copy-start | bytes 16
  324.5 21.9 %copy-start.16 = (s32[8]{0:T(128)S(1)}, s32[8]{0:T(128)}, u32[]{:S(2)}) copy-start(s32[8]{0:T(128)} %fusion.23) | copy-start | bytes 100
  342.7 3.7 collective-permute-start.18
  342.8 3.7 collective-permute-start.19
  344.2 4.5 collective-permute-start.20
  348.9 5.1 collective-permute-start.21
  348.9 5.1 collective-permute-start.22
  350.6 7.0 %collective-permute-start.23 = (bf16[8464]{0:T(1024)(128)(2,1)S(1)}, bf16[8464]{0:T(1024)(128)(2,1)S(1)}, u32[]{:S(2)}, u32[]{:S(2)}) collective-permute-start(bf16[8464]{0:T(1024)(128)(2,1)S(1)} %concatenate.75), channel_id=1, source_target_pairs={{0,12},{1,13},{2,14},{3,15},{4,8},{5,9},{6,10},{7,11},{8,4},{9,5},... | collective-permute-start | bytes 50792 | tf_op jit(solution)/shard_map/ppermute | solution.py:455
  351.4 6.4 %collective-permute-start.24 = (bf16[8464]{0:T(1024)(128)(2,1)S(1)}, bf16[8464]{0:T(1024)(128)(2,1)S(1)}, u32[]{:S(2)}, u32[]{:S(2)}) collective-permute-start(bf16[8464]{0:T(1024)(128)(2,1)S(1)} %concatenate.75), channel_id=1, source_target_pairs={{0,16},{1,17},{2,18},{3,19},{4,20},{5,21},{6,22},{7,23},{8,24},{9,... | collective-permute-start | bytes 50792 | tf_op jit(solution)/shard_map/ppermute | solution.py:455
  354.0 4.3 collective-permute-start.25
  354.0 5.7 %collective-permute-start.26 = (bf16[8464]{0:T(1024)(128)(2,1)S(1)}, bf16[8464]{0:T(1024)(128)(2,1)S(1)}, u32[]{:S(2)}, u32[]{:S(2)}) collective-permute-start(bf16[8464]{0:T(1024)(128)(2,1)S(1)} %concatenate.75), channel_id=1, source_target_pairs={{0,24},{1,25},{2,26},{3,27},{4,28},{5,29},{6,30},{7,31},{8,16},{9,... | collective-permute-start | bytes 50792 | tf_op jit(solution)/shard_map/ppermute | solution.py:455
  357.6 5.0 collective-permute-start.27
  357.8 19.5 %collective-permute-start.28 = (bf16[4,576,384]{2,1,0:T(8,128)(2,1)}, bf16[4,576,384]{2,1,0:T(8,128)(2,1)}, u32[]{:S(2)}, u32[]{:S(2)}) collective-permute-start(bf16[4,576,384]{2,1,0:T(8,128)(2,1)} %get-tuple-element.97), channel_id=1, source_target_pairs={{0,4},{1,5},{2,6},{3,7},{4,0},{5,1},{6,2},{7,3},{8,12},{9,13},{10,... | collective-permute-start | bytes 5308424 | tf_op jit(solution)/shard_map/ppermute | solution.py:455
  370.8 32.4 %collective-permute-start.39 = (bf16[2,1728,384]{2,1,0:T(8,128)(2,1)}, bf16[2,1728,384]{2,1,0:T(8,128)(2,1)}, u32[]{:S(2)}, u32[]{:S(2)}) collective-permute-start(bf16[2,1728,384]{2,1,0:T(8,128)(2,1)} %get-tuple-element.116), channel_id=1, source_target_pairs={{0,2},{1,3},{2,0},{3,1},{4,5},{5,4},{6,7},{7,6},{8,10},{9,11},{10,... | collective-permute-start | bytes 7962632 | tf_op jit(solution)/shard_map/ppermute | solution.py:455
  380.7 36.1 %collective-permute-start.29 = (bf16[2,576,384]{2,1,0:T(8,128)(2,1)}, bf16[2,576,384]{2,1,0:T(8,128)(2,1)}, u32[]{:S(2)}, u32[]{:S(2)}) collective-permute-start(bf16[2,576,384]{2,1,0:T(8,128)(2,1)} %get-tuple-element.118), channel_id=1, source_target_pairs={{0,2},{1,3},{2,0},{3,1},{4,5},{5,4},{6,7},{7,6},{8,10},{9,11},{10,... | collective-permute-start | bytes 2654216 | tf_op jit(solution)/shard_map/ppermute | solution.py:455
  403.2 17.1 %copy-start.6 = (bf16[1,4,1540]{2,1,0:T(4,128)(2,1)S(1)}, bf16[1,4,1540]{2,1,0:T(4,128)(2,1)}, u32[]{:S(2)}) copy-start(bf16[1,4,1540]{2,1,0:T(4,128)(2,1)} %stack_reshape.63) | copy-start | bytes 36964
  405.9 42.2 %collective-permute-start.40 = (bf16[1,1728,384]{2,1,0:T(8,128)(2,1)}, bf16[1,1728,384]{2,1,0:T(8,128)(2,1)}, u32[]{:S(2)}, u32[]{:S(2)}) collective-permute-start(bf16[1,1728,384]{2,1,0:T(8,128)(2,1)} %add_convert_fusion.3), channel_id=1, source_target_pairs={{0,1},{1,0},{2,3},{3,2},{4,6},{5,7},{6,4},{7,5},{8,9},{9,8},{10,11... | collective-permute-start | bytes 3981320 | tf_op jit(solution)/shard_map/ppermute | solution.py:455
  417.9 13.0 %collective-permute-start.30 = (bf16[1,576,384]{2,1,0:T(8,128)(2,1)S(1)}, bf16[1,576,384]{2,1,0:T(8,128)(2,1)S(1)}, u32[]{:S(2)}, u32[]{:S(2)}) collective-permute-start(bf16[1,576,384]{2,1,0:T(8,128)(2,1)S(1)} %add_convert_fusion.8), channel_id=1, source_target_pairs={{0,1},{1,0},{2,3},{3,2},{4,6},{5,7},{6,4},{7,5},{8,9},{9,8},{10,11... | collective-permute-start | bytes 1327112 | tf_op jit(solution)/shard_map/ppermute | solution.py:455
  432.9 6.5 %collective-permute-start.31 = (bf16[144,384]{1,0:T(8,128)(2,1)S(1)}, bf16[144,384]{1,0:T(8,128)(2,1)S(1)}, u32[]{:S(2)}, u32[]{:S(2)}) collective-permute-start(bf16[144,384]{1,0:T(8,128)(2,1)S(1)} %get-tuple-element.136), channel_id=1, source_target_pairs={{0,8},{1,9},{2,10},{3,11},{4,12},{5,13},{6,14},{7,15},{8,0},{9,1},... | collective-permute-start | bytes 331784 | tf_op jit(solution)/shard_map/ppermute | solution.py:455
  433.0 11.6 %collective-permute-start.32 = (bf16[144,384]{1,0:T(8,128)(2,1)S(1)}, bf16[144,384]{1,0:T(8,128)(2,1)S(1)}, u32[]{:S(2)}, u32[]{:S(2)}) collective-permute-start(bf16[144,384]{1,0:T(8,128)(2,1)S(1)} %get-tuple-element.138), channel_id=1, source_target_pairs={{0,16},{1,17},{2,18},{3,19},{4,20},{5,21},{6,22},{7,23},{8,24},{9,... | collective-permute-start | bytes 331784 | tf_op jit(solution)/shard_map/ppermute | solution.py:455
  434.1 10.6 %collective-permute-start.33 = (bf16[144,384]{1,0:T(8,128)(2,1)S(1)}, bf16[144,384]{1,0:T(8,128)(2,1)S(1)}, u32[]{:S(2)}, u32[]{:S(2)}) collective-permute-start(bf16[144,384]{1,0:T(8,128)(2,1)S(1)} %get-tuple-element.137), channel_id=1, source_target_pairs={{0,24},{1,25},{2,26},{3,27},{4,28},{5,29},{6,30},{7,31},{8,16},{9,... | collective-permute-start | bytes 331784 | tf_op jit(solution)/shard_map/ppermute | solution.py:455
  445.7 10.8 %collective-permute-start.34 = (bf16[144,384]{1,0:T(8,128)(2,1)S(1)}, bf16[144,384]{1,0:T(8,128)(2,1)S(1)}, u32[]{:S(2)}, u32[]{:S(2)}) collective-permute-start(bf16[144,384]{1,0:T(8,128)(2,1)S(1)} %get-tuple-element.114), channel_id=1, source_target_pairs={{0,8},{1,9},{2,10},{3,11},{4,12},{5,13},{6,14},{7,15},{8,0},{9,1},... | collective-permute-start | bytes 331784 | tf_op jit(solution)/shard_map/ppermute | solution.py:455
  450.5 14.7 %collective-permute-start.41 = (bf16[432,384]{1,0:T(8,128)(2,1)S(1)}, bf16[432,384]{1,0:T(8,128)(2,1)S(1)}, u32[]{:S(2)}, u32[]{:S(2)}) collective-permute-start(bf16[432,384]{1,0:T(8,128)(2,1)S(1)} %get-tuple-element.125), channel_id=1, source_target_pairs={{0,8},{1,9},{2,10},{3,11},{4,12},{5,13},{6,14},{7,15},{8,0},{9,1},... | collective-permute-start | bytes 995336 | tf_op jit(solution)/shard_map/ppermute | solution.py:455
  450.6 30.7 %collective-permute-start.42 = (bf16[432,384]{1,0:T(8,128)(2,1)S(1)}, bf16[432,384]{1,0:T(8,128)(2,1)S(1)}, u32[]{:S(2)}, u32[]{:S(2)}) collective-permute-start(bf16[432,384]{1,0:T(8,128)(2,1)S(1)} %get-tuple-element.127), channel_id=1, source_target_pairs={{0,16},{1,17},{2,18},{3,19},{4,20},{5,21},{6,22},{7,23},{8,24},{9,... | collective-permute-start | bytes 995336 | tf_op jit(solution)/shard_map/ppermute | solution.py:455
  452.5 28.7 %collective-permute-start.43 = (bf16[432,384]{1,0:T(8,128)(2,1)S(1)}, bf16[432,384]{1,0:T(8,128)(2,1)S(1)}, u32[]{:S(2)}, u32[]{:S(2)}) collective-permute-start(bf16[432,384]{1,0:T(8,128)(2,1)S(1)} %get-tuple-element.126), channel_id=1, source_target_pairs={{0,24},{1,25},{2,26},{3,27},{4,28},{5,29},{6,30},{7,31},{8,16},{9,... | collective-permute-start | bytes 995336 | tf_op jit(solution)/shard_map/ppermute | solution.py:455
  456.5 33.8 %collective-permute-start.35 = (bf16[144,384]{1,0:T(8,128)(2,1)S(1)}, bf16[144,384]{1,0:T(8,128)(2,1)S(1)}, u32[]{:S(2)}, u32[]{:S(2)}) collective-permute-start(bf16[144,384]{1,0:T(8,128)(2,1)S(1)} %get-tuple-element.114), channel_id=1, source_target_pairs={{0,16},{1,17},{2,18},{3,19},{4,20},{5,21},{6,22},{7,23},{8,24},{9,... | collective-permute-start | bytes 331784 | tf_op jit(solution)/shard_map/ppermute | solution.py:455
  456.5 33.9 %collective-permute-start.36 = (bf16[144,384]{1,0:T(8,128)(2,1)S(1)}, bf16[144,384]{1,0:T(8,128)(2,1)S(1)}, u32[]{:S(2)}, u32[]{:S(2)}) collective-permute-start(bf16[144,384]{1,0:T(8,128)(2,1)S(1)} %get-tuple-element.114), channel_id=1, source_target_pairs={{0,24},{1,25},{2,26},{3,27},{4,28},{5,29},{6,30},{7,31},{8,16},{9,... | collective-permute-start | bytes 331784 | tf_op jit(solution)/shard_map/ppermute | solution.py:455
  481.4 33.1 %copy-start.7 = (f32[1,2304]{1,0:T(1,128)S(1)}, f32[1,2304]{1,0:T(1,128)}, u32[]{:S(2)}) copy-start(f32[1,2304]{1,0:T(1,128)} %fusion.12) | copy-start | bytes 27652
  481.6 18.6 %collective-permute-start.44 = (bf16[432,384]{1,0:T(8,128)(2,1)S(1)}, bf16[432,384]{1,0:T(8,128)(2,1)S(1)}, u32[]{:S(2)}, u32[]{:S(2)}) collective-permute-start(bf16[432,384]{1,0:T(8,128)(2,1)S(1)} %get-tuple-element.112), channel_id=1, source_target_pairs={{0,8},{1,9},{2,10},{3,11},{4,12},{5,13},{6,14},{7,15},{8,0},{9,1},... | collective-permute-start | bytes 995336 | tf_op jit(solution)/shard_map/ppermute | solution.py:455
  490.3 23.9 %collective-permute-start.45 = (bf16[432,384]{1,0:T(8,128)(2,1)S(1)}, bf16[432,384]{1,0:T(8,128)(2,1)S(1)}, u32[]{:S(2)}, u32[]{:S(2)}) collective-permute-start(bf16[432,384]{1,0:T(8,128)(2,1)S(1)} %get-tuple-element.112), channel_id=1, source_target_pairs={{0,16},{1,17},{2,18},{3,19},{4,20},{5,21},{6,22},{7,23},{8,24},{9,... | collective-permute-start | bytes 995336 | tf_op jit(solution)/shard_map/ppermute | solution.py:455
  490.4 25.3 %collective-permute-start.37 = (bf16[576,384]{1,0:T(8,128)(2,1)S(1)}, bf16[576,384]{1,0:T(8,128)(2,1)S(1)}, u32[]{:S(2)}, u32[]{:S(2)}) collective-permute-start(bf16[576,384]{1,0:T(8,128)(2,1)S(1)} %bitcast.101), channel_id=1, source_target_pairs={{0,4},{1,5},{2,6},{3,7},{4,0},{5,1},{6,2},{7,3},{8,12},{9,13},{10,... | collective-permute-start | bytes 1327112 | tf_op jit(solution)/shard_map/ppermute | solution.py:455
  490.5 23.8 %collective-permute-start.46 = (bf16[432,384]{1,0:T(8,128)(2,1)S(1)}, bf16[432,384]{1,0:T(8,128)(2,1)S(1)}, u32[]{:S(2)}, u32[]{:S(2)}) collective-permute-start(bf16[432,384]{1,0:T(8,128)(2,1)S(1)} %get-tuple-element.112), channel_id=1, source_target_pairs={{0,24},{1,25},{2,26},{3,27},{4,28},{5,29},{6,30},{7,31},{8,16},{9,... | collective-permute-start | bytes 995336 | tf_op jit(solution)/shard_map/ppermute | solution.py:455
  514.3 4.2 collective-permute-start.47
  (7 other events, 19.7 us)
